TPU v7x, 32 devices: a whole 2x2x4 slice. The times are simulated.
32 devices in a mesh: rep: 2 (over y), grp: 4 (over z), sub: 4 (over x, core).
Axes of the slice: x: 2, y: 2, z: 4, core: 2. Of those that a mesh axis runs over, the one named last changes fastest.
Arguments:
- embeddings: bfloat16 [8192, 1024], P(('rep', 'grp', 'sub')), parts along dimension 0, may hold values from -6 to 6
- cluster_ids: int32 [8192, 1], P(('rep', 'grp', 'sub')), parts along dimension 0, may hold values from 0 to 3; in each aligned block of 256 rows (0 to 255, 256 to 511, ...) at most 128 rows name the same one
Outputs:
- max_similarity: float32 [8192], P(('rep', 'grp', 'sub')), parts along dimension 0
There are 2 independent parts, one for each index of `rep`. A program takes and returns all parts, laid end to end along the dimension named above; each array names one. Nothing has to cross between parts.
Inputs may be any that keep to these rules, and one draw needn't show every extreme that they name: `cluster_ids`: cluster numbers run from 0 to 3; among the rows of one device no cluster is named by more than 128 rows, and in every draw some cluster is named by exactly 128 rows of some device.
All inputs are finite; a program needn't handle non-finite values.
Results may differ from a plain program's by a relative error of at most 0.0014.
Values may be sent and summed in bfloat16 or wider, within the bound.
A program may use at most 64 MiB of HBM per device.

v0:
```python
import functools
import math

import jax
import jax.numpy as jnp
from jax import lax
from jax.experimental import pallas as pl
from jax.experimental.pallas import tpu as pltpu
from jax.sharding import PartitionSpec as P

LANES = 128
SUBLANES = 8
VMEM_BUDGET = 24 << 20
MESH = pl.DeviceIdType.MESH


def from_behind(value, axis, by):
    peers = lax.axis_size(axis)
    return lax.ppermute(value, axis, [(i, (i + by) % peers) for i in range(peers)])


def masked_maxima(left_rows, right_rows, right_present, excluded):
    similar = jnp.dot(left_rows, right_rows.T, preferred_element_type=jnp.float32)
    allowed = (right_present[None, :] > 0) & jnp.logical_not(excluded)
    return jnp.where(allowed, similar, jnp.float32(-1.0))


def unit_of(rows, features):
    floats = rows.astype(jnp.float32)
    return (
        floats
        * lax.rsqrt(jnp.mean(floats * floats, axis=1, keepdims=True) + 1e-06)
        / math.sqrt(features)
    ).astype(jnp.bfloat16)


def by_owner(embeddings, cluster_ids):
    rows_dev, features = embeddings.shape
    groups = lax.axis_size("grp")
    subgroup = lax.axis_size("sub")
    capacity = 2 * rows_dev // groups
    unit_rows = unit_of(embeddings, features)
    labels = cluster_ids[:, 0]
    member_table = (labels[:, None] == jnp.arange(groups, dtype=jnp.int32)[None, :]).astype(
        jnp.int32
    )
    running = jnp.cumsum(member_table, axis=0)
    within = jnp.sum(jnp.where(member_table > 0, running - 1, 0), axis=1)
    slot_index = labels * capacity + within
    outgoing = jnp.zeros((groups * capacity, features), jnp.bfloat16).at[slot_index].set(unit_rows)
    occupied = jnp.zeros((groups * capacity,), jnp.int32).at[slot_index].set(1)
    arrived, arrived_present = (
        lax.all_to_all(
            outgoing.reshape(groups, capacity, features),
            "grp",
            split_axis=0,
            concat_axis=0,
            tiled=True,
        ),
        lax.all_to_all(
            occupied.reshape(groups, capacity), "grp", split_axis=0, concat_axis=0, tiled=True
        ),
    )
    owned_rows = arrived.reshape(groups * capacity, features)
    present = arrived_present.reshape(groups * capacity)
    held = owned_rows.shape[0]
    positions = jnp.arange(held, dtype=jnp.int32)
    excluded = positions[:, None] == positions[None, :]
    highest = jnp.max(masked_maxima(owned_rows, owned_rows, present, excluded), axis=1)
    no_exclusion = jnp.zeros((held, held), dtype=bool)
    for offset in range(1, subgroup // 2 + 1):
        peer_rows, peer_present = from_behind((owned_rows, present), "sub", offset)
        scores = masked_maxima(owned_rows, peer_rows, peer_present, no_exclusion)
        highest = jnp.maximum(highest, jnp.max(scores, axis=1))
        if 2 * offset != subgroup:
            column_best = jnp.max(
                jnp.where(present[:, None] > 0, scores, jnp.float32(-1.0)), axis=0
            )
            returned_best = from_behind(column_best, "sub", -offset)
            highest = jnp.maximum(highest, returned_best)
    returned = lax.all_to_all(
        highest.reshape(groups, capacity), "grp", split_axis=0, concat_axis=0, tiled=True
    )
    return returned.reshape(groups * capacity)[slot_index]


def meet_kernel(
    groups, subgroup, chunks,
    emb_ref, ids_ref, out_ref,
    level, foreign, relay, lane_ids, level_ids, ids_col, row_part, col_part,
    ret_out, ret_in, col_out, col_in,
    ids_send, ids_recv, lid_send, lid_recv, lvl_send, lvl_recv, fwd_send,
    z_send, z_recv, out_send, relay_send, relay_recv, ret_send, ret_recv, col_send, col_recv,
):
    rows, features = emb_ref.shape
    size = rows // chunks
    pivot = groups // 2
    rep = lax.axis_index("rep")
    depth = lax.axis_index("grp")
    z = depth * (1 - rep) + (groups - 1 - depth) * rep
    s = lax.axis_index("sub")
    partner = s + 1 - 2 * lax.rem(s, 2)
    others = subgroup // 2
    odd = lax.rem(s, 2) == 1
    even = lax.rem(s, 2) == 0
    relay_at = groups - 1 - z
    across_y = {"rep": 1 - rep}

    def peer(k):
        return lax.rem(s + k, subgroup)

    def lane(k):
        return lax.rem(z + k, groups)

    def at(where):
        return {"grp": where * (1 - rep) + (groups - 1 - where) * rep}

    barrier = pltpu.get_barrier_semaphore()
    for k in range(1, subgroup):
        pl.semaphore_signal(barrier, 1, device_id={"sub": peer(k)}, device_id_type=MESH)
    for k in range(1, groups):
        pl.semaphore_signal(barrier, 1, device_id=at(lane(k)), device_id_type=MESH)

    pl.semaphore_signal(barrier, 1, device_id=across_y, device_id_type=MESH)

    def slot(b):
        return pl.ds(pl.multiple_of(b * rows, rows), rows)

    def piece(b, k):
        return pl.ds(pl.multiple_of(b * rows + k * size, size), size)

    def part(k):
        return pl.ds(pl.multiple_of(k * size, size), size)

    def normalize(k, carry):
        level[piece(s, k), :] = unit_of(emb_ref[part(k), :], features)
        return carry

    lax.fori_loop(0, chunks, normalize, 0)
    level_ids[s] = ids_ref[...]
    lane_ids[z] = ids_ref[...]
    col_part[...] = jnp.full(col_part.shape, -1.0, jnp.float32)
    pl.semaphore_wait(barrier, subgroup + groups - 1)

    def remote(src, dst, send, recv, where):
        return pltpu.make_async_remote_copy(
            src_ref=src, dst_ref=dst, send_sem=send, recv_sem=recv,
            device_id=where, device_id_type=MESH,
        )

    def level_ids_copy(k, owner):
        return remote(ids_ref, level_ids.at[owner], lid_send.at[k], lid_recv.at[owner], {"sub": peer(k)})

    def lane_ids_copy(k, owner):
        return remote(ids_ref, lane_ids.at[owner], ids_send.at[k], ids_recv.at[owner], at(lane(k)))

    def own_to_lane(k, where):
        return remote(
            level.at[piece(s, k), :], foreign.at[z, part(k), :], z_send.at[z, k], z_recv.at[z, k],
            at(where),
        )

    def passed_on(i, k, where):
        block = foreign.at[i, part(k), :]
        return remote(block, block, z_send.at[i, k], z_recv.at[i, k], at(where))

    def own_across(k):
        return remote(
            level.at[piece(s, k), :], relay.at[z, part(k), :], out_send.at[k], relay_recv.at[z, k],
            across_y,
        )

    def relayed(i, k):
        block = relay.at[i, part(k), :]
        return remote(block, block, relay_send.at[i, k], relay_recv.at[i, k], at(z - 1))

    def passed_across(i, k):
        return remote(
            foreign.at[i, part(k), :], relay.at[i, part(k), :], z_send.at[i, k], relay_recv.at[i, k],
            across_y,
        )

    def back_across(i, k):
        return remote(
            relay.at[i, part(k), :], foreign.at[i, part(k), :], relay_send.at[i, k], z_recv.at[i, k],
            across_y,
        )

    def block_to_peer(owner, send, where):
        block = level.at[slot(owner), :]
        return remote(block, block, send, lvl_recv.at[owner], {"sub": where})

    for k in range(1, groups):
        lane_ids_copy(k, z).start()
    for k in range(1, subgroup):
        level_ids_copy(k, s).start()

    at_bank = odd & (z == pivot - 1)
    sends_right = (z < pivot) & (even | (z < pivot - 1))
    sends_left = z > pivot

    @pl.when(at_bank)
    def _():
        lax.fori_loop(0, chunks, lambda k, c: (own_across(k).start(), c)[1], 0)

    @pl.when(sends_right)
    def _():
        lax.fori_loop(0, chunks, lambda k, c: (own_to_lane(k, z + 1).start(), c)[1], 0)

    @pl.when(sends_left)
    def _():
        lax.fori_loop(0, chunks, lambda k, c: (own_to_lane(k, z - 1).start(), c)[1], 0)

    for k in range(1, others):
        block_to_peer(s, lvl_send.at[k], peer(2 * k)).start()
    block_to_peer(s, lvl_send.at[0], partner).start()

    def visits(i):
        return z > i if i < pivot else (z >= pivot) & (z < i)

    turned = lax.rem(s, 2) * (z // (pivot + 1))

    def passes(i):
        if i >= pivot:
            return (z > pivot) & (z < i)
        if i % 2 == 0:
            return (z > i) & (z < groups - 1) & (even | (z < pivot - 1) | (z > pivot - 1))
        return (z > i) & ((even & (z < groups - 1)) | (odd & ((z < pivot - 1) | (z > pivot))))

    def onward(i):
        if i >= pivot:
            return z - 1
        return z + 1 if i % 2 == 0 else z + 1 - 2 * turned

    def take(i):
        def one(k, carry):
            passed_on(i, k, z).wait_recv()

            @pl.when(passes(i))
            def _():
                passed_on(i, k, onward(i)).start()

            return carry

        lax.fori_loop(0, chunks, one, 0)

    last_stop = [pivot if i % 2 == 0 else groups - 1 for i in range(pivot)]

    def relays(i):
        return odd & (relay_at >= pivot - 1) & (relay_at <= last_stop[i])

    def relay_on(i, k):
        @pl.when(relays(i))
        def _():
            relayed(i, k).wait_recv()

            @pl.when(relay_at < last_stop[i])
            def _():
                relayed(i, k).start()

            @pl.when(relay_at == last_stop[i])
            def _():
                back_across(i, k).start()

    for i in range(pivot - 1, -1, -1):
        def relay_step(k, carry, i=i):
            relay_on(i, k)
            if i > 0:
                @pl.when(at_bank)
                def _():
                    passed_on(i - 1, k, z).wait_recv()
                    passed_across(i - 1, k).start()

            return carry

        @pl.when(odd)
        def _(relay_step=relay_step):
            lax.fori_loop(0, chunks, relay_step, 0)

    def soon(i):
        if i >= pivot:
            return visits(i)
        if i % 2 == 0:
            return visits(i) & (z <= pivot)
        return visits(i) & (even | (z < pivot) | (z == groups - 1))

    def later(i):
        if i % 2 == 0:
            return z > pivot
        return odd & (z >= pivot) & (z < groups - 1)

    sources = list(range(pivot - 1, -1, -1)) + list(range(pivot + 1, groups))

    def take_soon(mine):
        for i in sources:
            @pl.when(soon(i) & mine & (even | (z < pivot - 1) | (z > pivot - 1)) if i < pivot else soon(i) & mine)
            def _(i=i):
                take(i)

    take_soon(even)
    for k in range(1, others):
        came_from = peer(2 * k)
        block_to_peer(came_from, lvl_send.at[0], s).wait_recv()
        block_to_peer(came_from, fwd_send.at[k], partner).start()
    for k in range(0, others):
        came_from = lax.rem(partner + 2 * k, subgroup)
        block_to_peer(came_from, lvl_send.at[0], s).wait_recv()

    take_soon(odd)
    for k in range(1, groups):
        lane_ids_copy(k, lane(k)).wait_recv()
    for k in range(1, subgroup):
        level_ids_copy(k, peer(k)).wait_recv()
    for i in range(groups):
        ids_col[i] = jnp.broadcast_to(lane_ids[i], (LANES, rows)).T

    width = subgroup * rows

    def meet(block, i, own):
        similar = lax.dot_general(
            block, level[...], (((1,), (1,)), ((), ())), preferred_element_type=jnp.float32
        )
        own_ids = ids_col[i]
        best = jnp.full((rows, LANES), -1.0, jnp.float32)
        for col in range(0, width, LANES):
            same = own_ids == level_ids[col // rows, :, col % rows : col % rows + LANES]
            if own:
                across = lax.broadcasted_iota(jnp.int32, (rows, LANES), 1) + col
                down = lax.broadcasted_iota(jnp.int32, (rows, LANES), 0) + s * rows
                same = same & (across != down)
            kept = jnp.where(same, similar[:, col : col + LANES], jnp.float32(-1.0))
            best = jnp.maximum(best, kept)
            if not own:
                columns = jnp.max(kept.reshape(rows // SUBLANES, SUBLANES, LANES), axis=0)
                col_part[:, col : col + LANES] = jnp.maximum(col_part[:, col : col + LANES], columns)
        row_part[i] = best

    meet(level[slot(s), :], z, True)
    for i in sources:
        @pl.when(soon(i))
        def _(i=i):
            meet(foreign[i], i, False)

    for i in range(pivot):
        @pl.when(later(i))
        def _(i=i):
            take(i)
            meet(foreign[i], i, False)

    def flat(i):
        return jnp.max(row_part[i].T, axis=0, keepdims=True)

    def ret_copy(i, owner, where):
        return remote(ret_out.at[i], ret_in.at[owner], ret_send.at[i], ret_recv.at[owner], at(where))

    def col_copy(k, owner):
        return remote(col_out.at[peer(k)], col_in.at[owner], col_send.at[k], col_recv.at[owner], {"sub": peer(k)})

    for i in sources:
        @pl.when(visits(i))
        def _(i=i):
            ret_out[i] = flat(i)

    for b in range(subgroup):
        col_out[b] = jnp.max(col_part[:, b * rows : (b + 1) * rows], axis=0, keepdims=True)
    for i in sources:
        @pl.when(visits(i))
        def _(i=i):
            ret_copy(i, z, i).start()
    for k in range(1, subgroup):
        col_copy(k, s).start()

    out_ref[...] = jnp.maximum(flat(z), col_out[s])
    for k in range(1, subgroup):
        col_copy(k, peer(k)).wait_recv()
        out_ref[...] = jnp.maximum(out_ref[...], col_in[peer(k)])
    for j in range(1, groups):
        @pl.when((z < j) & (z < pivot) | (z > j) & (z > pivot) & (j >= pivot))
        def _(j=j):
            ret_copy(0, j, z).wait_recv()
            out_ref[...] = jnp.maximum(out_ref[...], ret_in[j])

    for k in range(1, groups):
        lane_ids_copy(k, z).wait_send()
    for k in range(1, subgroup):
        level_ids_copy(k, s).wait_send()
        col_copy(k, s).wait_send()
    for k in range(1, others):
        block_to_peer(s, lvl_send.at[k], peer(2 * k)).wait_send()
        block_to_peer(peer(2 * k), fwd_send.at[k], partner).wait_send()
    block_to_peer(s, lvl_send.at[0], partner).wait_send()

    @pl.when(at_bank)
    def _():
        lax.fori_loop(0, chunks, lambda k, c: (own_across(k).wait_send(), c)[1], 0)

    for i in range(pivot):
        @pl.when(relays(i))
        def _(i=i):
            lax.fori_loop(0, chunks, lambda k, c: (relayed(i, k).wait_send(), c)[1], 0)

    @pl.when(sends_right | sends_left)
    def _():
        lax.fori_loop(0, chunks, lambda k, c: (own_to_lane(k, z).wait_send(), c)[1], 0)

    for i in sources:
        @pl.when(passes(i))
        def _(i=i):
            lax.fori_loop(0, chunks, lambda k, c: (passed_on(i, k, z).wait_send(), c)[1], 0)

        if i < pivot - 1:
            @pl.when(at_bank)
            def _(i=i):
                lax.fori_loop(0, chunks, lambda k, c: (passed_across(i, k).wait_send(), c)[1], 0)

        @pl.when(visits(i))
        def _(i=i):
            ret_copy(i, z, i).wait_send()


def by_meeting(embeddings, cluster_ids, chunks):
    rows, features = embeddings.shape
    groups = lax.axis_size("grp")
    subgroup = lax.axis_size("sub")
    dma = pltpu.SemaphoreType.DMA
    best = pl.pallas_call(
        functools.partial(meet_kernel, groups, subgroup, chunks),
        out_shape=jax.ShapeDtypeStruct((1, rows), jnp.float32),
        in_specs=[pl.BlockSpec(memory_space=pltpu.VMEM)] * 2,
        out_specs=pl.BlockSpec(memory_space=pltpu.VMEM),
        scratch_shapes=[
            pltpu.VMEM((subgroup * rows, features), jnp.bfloat16),
            pltpu.VMEM((groups, rows, features), jnp.bfloat16),
            pltpu.VMEM((groups // 2, rows, features), jnp.bfloat16),
            pltpu.VMEM((groups, 1, rows), jnp.int32),
            pltpu.VMEM((subgroup, 1, rows), jnp.int32),
            pltpu.VMEM((groups, rows, LANES), jnp.int32),
            pltpu.VMEM((groups, rows, LANES), jnp.float32),
            pltpu.VMEM((SUBLANES, subgroup * rows), jnp.float32),
            pltpu.VMEM((groups, 1, rows), jnp.float32),
            pltpu.VMEM((groups, 1, rows), jnp.float32),
            pltpu.VMEM((subgroup, 1, rows), jnp.float32),
            pltpu.VMEM((subgroup, 1, rows), jnp.float32),
            dma((groups,)), dma((groups,)),
            dma((subgroup,)), dma((subgroup,)),
            dma((subgroup,)), dma((subgroup,)), dma((subgroup,)),
            dma((groups, chunks)), dma((groups, chunks)),
            dma((chunks,)), dma((groups // 2, chunks)), dma((groups // 2, chunks)),
            dma((groups,)), dma((groups,)),
            dma((subgroup,)), dma((subgroup,)),
        ],
        compiler_params=pltpu.CompilerParams(collective_id=0, has_side_effects=True),
    )(embeddings, cluster_ids.reshape(1, rows))
    return best.reshape(rows)


def local(embeddings, cluster_ids):
    rows, features = embeddings.shape
    groups = lax.axis_size("grp")
    subgroup = lax.axis_size("sub")
    held = (groups + subgroup) * rows * features * embeddings.dtype.itemsize
    chunks = max(1, rows // 32)
    paired = lax.axis_size("rep") == 2 and subgroup % 2 == 0 and groups // 2 == 2
    if held <= VMEM_BUDGET and paired and groups % 2 == 0 and rows % (LANES * 2) == 0:
        return by_meeting(embeddings, cluster_ids, chunks)
    return by_owner(embeddings, cluster_ids)


def solution(mesh):
    return jax.shard_map(
        local,
        mesh=mesh,
        in_specs=(P(("rep", "grp", "sub"), None), P(("rep", "grp", "sub"), None)),
        out_specs=P(("rep", "grp", "sub")),
        check_vma=False,
    )
```

profile of v0, /device:TPU:1, one launch (start us, length us, event | category | flops | bytes accessed | tf_op | source)
XLA Modules:
  0.0 37.8 jit_solution(3005204708452700887)
XLA Ops:
  0.0 36.5 %shard_map.28 = f32[1,256]{1,0:T(1,128)} custom-call(bf16[256,1024]{1,0:T(8,128)(2,1)} %emb_ref.1, s32[1,256]{1,0:T(1,128)} %bitcast.3), custom_call_target="tpu_custom_call" | custom-call | tf_op jit(solution)/shard_map/pallas_call | solution.py:426
  36.5 0.0 copy-start
  36.5 0.7 %copy-done = f32[1,256]{1,0:T(1,128)S(1)} copy-done((f32[1,256]{1,0:T(1,128)S(1)}, f32[1,256]{1,0:T(1,128)}, u32[]{:S(2)}) %copy-start) | copy-done | bytes 1048
  37.2 0.6 %copy.4 = f32[256]{0:T(256)} copy(f32[256]{0:T(256)S(1)} %bitcast.2) | data formatting | bytes 2048
Async XLA Ops:
  36.5 0.7 %copy-start = (f32[1,256]{1,0:T(1,128)S(1)}, f32[1,256]{1,0:T(1,128)}, u32[]{:S(2)}) copy-start(f32[1,256]{1,0:T(1,128)} %shard_map.28) | copy-start | bytes 3076
where the time goes:
time: 37.9 us; the launch traced here: 37.8 us
  Pallas kernels  36.5 us (96%)
  local copies, waits for them, and re-layouts  1.22 us (3%)
    pallas_call x1, Pallas kernels, by_meeting(): pl.pallas_call(functools.partial(meet_kernel, groups, subgroup, chunks),...  36.5 us
    unnamed x3, local copies, waits for them, and re-layouts  1.22 us

commit v1 on v0

v1 whole, which is shorter than its diff:
```python
import functools
import math

import jax
import jax.numpy as jnp
from jax import lax
from jax.experimental import pallas as pl
from jax.experimental.pallas import tpu as pltpu
from jax.sharding import PartitionSpec as P

LANES = 128
SUBLANES = 8
VMEM_BUDGET = 24 << 20
MESH = pl.DeviceIdType.MESH


def from_behind(value, axis, by):
    peers = lax.axis_size(axis)
    return lax.ppermute(value, axis, [(i, (i + by) % peers) for i in range(peers)])


def masked_maxima(left_rows, right_rows, right_present, excluded):
    similar = jnp.dot(left_rows, right_rows.T, preferred_element_type=jnp.float32)
    allowed = (right_present[None, :] > 0) & jnp.logical_not(excluded)
    return jnp.where(allowed, similar, jnp.float32(-1.0))


def unit_of(rows, features):
    floats = rows.astype(jnp.float32)
    return (
        floats
        * lax.rsqrt(jnp.mean(floats * floats, axis=1, keepdims=True) + 1e-06)
        / math.sqrt(features)
    ).astype(jnp.bfloat16)


def by_owner(embeddings, cluster_ids):
    rows_dev, features = embeddings.shape
    groups = lax.axis_size("grp")
    subgroup = lax.axis_size("sub")
    capacity = 2 * rows_dev // groups
    unit_rows = unit_of(embeddings, features)
    labels = cluster_ids[:, 0]
    member_table = (labels[:, None] == jnp.arange(groups, dtype=jnp.int32)[None, :]).astype(
        jnp.int32
    )
    running = jnp.cumsum(member_table, axis=0)
    within = jnp.sum(jnp.where(member_table > 0, running - 1, 0), axis=1)
    slot_index = labels * capacity + within
    outgoing = jnp.zeros((groups * capacity, features), jnp.bfloat16).at[slot_index].set(unit_rows)
    occupied = jnp.zeros((groups * capacity,), jnp.int32).at[slot_index].set(1)
    arrived, arrived_present = (
        lax.all_to_all(
            outgoing.reshape(groups, capacity, features),
            "grp",
            split_axis=0,
            concat_axis=0,
            tiled=True,
        ),
        lax.all_to_all(
            occupied.reshape(groups, capacity), "grp", split_axis=0, concat_axis=0, tiled=True
        ),
    )
    owned_rows = arrived.reshape(groups * capacity, features)
    present = arrived_present.reshape(groups * capacity)
    held = owned_rows.shape[0]
    positions = jnp.arange(held, dtype=jnp.int32)
    excluded = positions[:, None] == positions[None, :]
    highest = jnp.max(masked_maxima(owned_rows, owned_rows, present, excluded), axis=1)
    no_exclusion = jnp.zeros((held, held), dtype=bool)
    for offset in range(1, subgroup // 2 + 1):
        peer_rows, peer_present = from_behind((owned_rows, present), "sub", offset)
        scores = masked_maxima(owned_rows, peer_rows, peer_present, no_exclusion)
        highest = jnp.maximum(highest, jnp.max(scores, axis=1))
        if 2 * offset != subgroup:
            column_best = jnp.max(
                jnp.where(present[:, None] > 0, scores, jnp.float32(-1.0)), axis=0
            )
            returned_best = from_behind(column_best, "sub", -offset)
            highest = jnp.maximum(highest, returned_best)
    returned = lax.all_to_all(
        highest.reshape(groups, capacity), "grp", split_axis=0, concat_axis=0, tiled=True
    )
    return returned.reshape(groups * capacity)[slot_index]


def meet_kernel(
    groups, subgroup, chunks, pieces,
    emb_ref, ids_ref, out_ref,
    emb_in, level, foreign, relay, lane_ids, level_ids, ids_col, row_part, col_part,
    ret_out, ret_in, col_out, col_in,
    in_sem, ids_in, ids_send, ids_recv, lid_send, lid_recv,
    lvl_send, lvl_recv, fwd_send, own_send, z_send, z_recv,
    relay_send, relay_back, relay_recv, ret_send, ret_recv, col_send, col_recv,
):
    rows, features = emb_ref.shape
    size = rows // chunks
    load = rows // pieces
    share = chunks // 4
    pivot = groups // 2
    last = groups - 1
    rep = lax.axis_index("rep")
    depth = lax.axis_index("grp")
    z = depth * (1 - rep) + (last - depth) * rep
    s = lax.axis_index("sub")
    partner = s + 1 - 2 * lax.rem(s, 2)
    others = subgroup // 2
    across_y = {"rep": 1 - rep}

    def peer(k):
        return lax.rem(s + k, subgroup)

    def at(where):
        return {"grp": where * (1 - rep) + (last - where) * rep}

    def remote(src, dst, send, recv, where):
        return pltpu.make_async_remote_copy(
            src_ref=src, dst_ref=dst, send_sem=send, recv_sem=recv,
            device_id=where, device_id_type=MESH,
        )

    def slot(b):
        return pl.ds(pl.multiple_of(b * rows, rows), rows)

    def piece(b, p):
        return pl.ds(pl.multiple_of(b * rows + p * load, load), load)

    def own_chunk(k):
        return level.at[pl.ds(pl.multiple_of(s * rows + k * size, size), size), :]

    def part(k):
        return pl.ds(pl.multiple_of(k * size, size), size)

    def load_piece(p):
        where = pl.ds(pl.multiple_of(p * load, load), load)
        return pltpu.make_async_copy(emb_ref.at[where, :], emb_in.at[where, :], in_sem.at[p])

    for p in range(pieces):
        load_piece(p).start()
    ids_copy = pltpu.make_async_copy(ids_ref, level_ids.at[s], ids_in)
    ids_copy.start()

    barrier = pltpu.get_barrier_semaphore()
    for k in range(1, subgroup):
        pl.semaphore_signal(barrier, 1, device_id={"sub": peer(k)}, device_id_type=MESH)
    pl.semaphore_signal(barrier, 1, device_id=across_y, device_id_type=MESH)

    @pl.when(z > 0)
    def _():
        pl.semaphore_signal(barrier, 1, device_id=at(z - 1), device_id_type=MESH)

    @pl.when(z < last)
    def _():
        pl.semaphore_signal(barrier, 1, device_id=at(z + 1), device_id_type=MESH)

    col_part[...] = jnp.full(col_part.shape, -1.0, jnp.float32)

    def level_ids_copy(k, owner):
        return remote(ids_ref, level_ids.at[owner], lid_send.at[k], lid_recv.at[owner], {"sub": peer(k)})

    def own_ids(where):
        return remote(ids_ref, lane_ids.at[z], ids_send.at[z], ids_recv.at[z], at(where))

    def ids_on(i, where):
        return remote(lane_ids.at[i], lane_ids.at[i], ids_send.at[i], ids_recv.at[i], at(where))

    def own_along(k, where):
        return remote(own_chunk(k), foreign.at[z, part(k), :], own_send.at[k], z_recv.at[z, k], at(where))

    def own_across(k):
        return remote(own_chunk(k), relay.at[z, part(k), :], own_send.at[k], relay_recv.at[z, k], across_y)

    def passed_on(i, k, where):
        block = foreign.at[i, part(k), :]
        return remote(block, block, z_send.at[i, k], z_recv.at[i, k], at(where))

    def passed_across(i, k):
        return remote(
            foreign.at[i, part(k), :], relay.at[i, part(k), :], z_send.at[i, k], relay_recv.at[i, k],
            across_y,
        )

    def relayed(i, k):
        block = relay.at[i, part(k), :]
        return remote(block, block, relay_send.at[i, k], relay_recv.at[i, k], at(z - 1))

    def back_across(i, k):
        return remote(
            relay.at[i, part(k), :], foreign.at[i, part(k), :], relay_back.at[i, k], z_recv.at[i, k],
            across_y,
        )

    def level_piece(owner, p, send, where):
        block = level.at[piece(owner, p), :]
        return remote(block, block, send, lvl_recv.at[owner, p], {"sub": where})

    sends_right = z < pivot
    sends_left = z == last

    def start_own(k):
        @pl.when((z == 0) | (z == 1) & (k < 2 * share))
        def _():
            own_along(k, z + 1).start()

        @pl.when((z == 1) & (k >= 2 * share))
        def _():
            own_across(k).start()

        @pl.when(sends_left)
        def _():
            own_along(k, z - 1).start()

    step = 2 * size
    per_piece = load // step

    def normalize(h):
        where = pl.ds(pl.multiple_of(h * step, step), step)
        into = pl.ds(pl.multiple_of(s * rows + h * step, step), step)
        level[into, :] = unit_of(emb_in[where, :], features)

    def send_own(p):
        @pl.when(z != pivot)
        def _():
            lax.fori_loop(
                2 * per_piece * p, 2 * per_piece * (p + 1), lambda k, c: (start_own(k), c)[1], 0
            )

        for k in range(1, others):
            level_piece(s, p, lvl_send.at[k, p], peer(2 * k)).start()
        level_piece(s, p, lvl_send.at[0, p], partner).start()

    load_piece(0).wait()
    lax.fori_loop(0, per_piece, lambda h, c: (normalize(h), c)[1], 0)
    neighbours = subgroup + (z > 0).astype(jnp.int32) + (z < last).astype(jnp.int32)
    pl.semaphore_wait(barrier, neighbours)
    for k in range(1, subgroup):
        level_ids_copy(k, s).start()

    @pl.when(sends_right)
    def _():
        own_ids(z + 1).start()

    @pl.when(sends_left)
    def _():
        own_ids(z - 1).start()

    send_own(0)

    def norm_step(p, carry):
        load_piece(p).wait()
        lax.fori_loop(p * per_piece, (p + 1) * per_piece, lambda h, c: (normalize(h), c)[1], 0)
        send_own(p)
        return carry

    lax.fori_loop(1, pieces, norm_step, 0)
    ids_copy.wait()

    def level_forward(p):
        for k in range(1, others):
            came_from = peer(2 * k)
            level_piece(came_from, p, lvl_send.at[0, p], s).wait_recv()
            level_piece(came_from, p, fwd_send.at[k, p], partner).start()

    def relay_step(j):
        block = 1 - j // (2 * share)
        chunk = lax.rem(j + 2 * share, chunks)
        hold = relayed(block, chunk)
        hold.wait_recv()

        @pl.when(z > 0)
        def _():
            hold.start()

        @pl.when((z == 0) | (z == 1) & (j >= share))
        def _():
            back_across(block, chunk).start()

    crossing = 3 * share

    def ticks(count, native, lag_relay, lag_level, relays=True):
        def tick(t, carry):
            native(t)
            if relays:
                j = t - lag_relay

                @pl.when((j >= 0) & (j < crossing))
                def _():
                    relay_step(j)

            p = t - lag_level

            @pl.when((p >= 0) & (lax.rem(p, share) == 0) & (p < pieces * share))
            def _():
                level_forward(p // share)

            return carry

        lax.fori_loop(0, count, tick, 0)

    def wait_chunks(i, low, high):
        lax.fori_loop(low, high, lambda k, c: (passed_on(i, k, z).wait_recv(), c)[1], 0)

    @pl.when(z == 0)
    def _():
        ticks(share * 3 + 3 * share, lambda t: None, 0, 3 * rep)

    @pl.when(z == 1)
    def _():
        ids_on(0, z).wait_recv()
        ids_on(0, z + 1).start()

        def native(k):
            @pl.when(k < chunks)
            def _():
                passed_on(0, k, z).wait_recv()

                @pl.when(k < share)
                def _():
                    passed_across(0, k).start()

                @pl.when(k >= share)
                def _():
                    passed_on(0, k, z + 1).start()

        ticks(chunks + share, native, 4 * (1 - rep), 4 - 2 * rep)

    @pl.when(z == pivot)
    def _():
        ids_on(1, z).wait_recv()
        ids_on(1, z + 1).start()

        def native(k):
            @pl.when(k < 2 * share)
            def _():
                passed_on(1, k, z).wait_recv()
                passed_on(1, k, z + 1).start()

            @pl.when((k >= 2 * share) & (k < 5 * share))
            def _():
                passed_on(0, k - share, z).wait_recv()
                passed_on(0, k - share, z + 1).start()

        ticks(5 * share, native, 0, 4)
        ids_on(0, z).wait_recv()
        ids_on(0, z + 1).start()
        ids_on(last, z).wait_recv()

    @pl.when(z == last)
    def _():
        def native(t):
            k = t + share

            @pl.when((t >= share) & (t < 2 * share))
            def _():
                passed_on(1, k, z).wait_recv()
                passed_on(1, k, z - 1).start()

        ticks(4 * share, native, 0, 0, relays=False)
        ids_on(0, z).wait_recv()
        ids_on(1, z).wait_recv()

    for p in range(pieces):
        for k in range(0, others):
            level_piece(lax.rem(partner + 2 * k, subgroup), p, lvl_send.at[0, p], s).wait_recv()
    for k in range(1, subgroup):
        level_ids_copy(k, peer(k)).wait_recv()

    def spread(i, ids):
        ids_col[i] = jnp.broadcast_to(ids, (LANES, rows)).T

    spread(z, level_ids[s])
    width = subgroup * rows

    def meet(i, low, high, own):
        count = high - low
        block = level[slot(s), :] if own else foreign[i, low:high, :]
        similar = lax.dot_general(
            block, level[...], (((1,), (1,)), ((), ())), preferred_element_type=jnp.float32
        )
        own_ids = ids_col[i, low:high, :]
        best = jnp.full((count, LANES), -1.0, jnp.float32)
        for col in range(0, width, LANES):
            same = own_ids == level_ids[col // rows, :, col % rows : col % rows + LANES]
            if own:
                across = lax.broadcasted_iota(jnp.int32, (rows, LANES), 1) + col
                down = lax.broadcasted_iota(jnp.int32, (rows, LANES), 0) + s * rows
                same = same & (across != down)
            kept = jnp.where(same, similar[:, col : col + LANES], jnp.float32(-1.0))
            best = jnp.maximum(best, kept)
            if not own:
                columns = jnp.max(kept.reshape(count // SUBLANES, SUBLANES, LANES), axis=0)
                col_part[:, col : col + LANES] = jnp.maximum(col_part[:, col : col + LANES], columns)
        row_part[i, low:high, :] = best

    def flat(i):
        return jnp.max(row_part[i].T, axis=0, keepdims=True)

    def ret_copy(i, owner, where):
        return remote(ret_out.at[i], ret_in.at[owner], ret_send.at[i], ret_recv.at[owner], at(where))

    def col_copy(k, owner):
        return remote(col_out.at[peer(k)], col_in.at[owner], col_send.at[k], col_recv.at[owner], {"sub": peer(k)})

    def give(i):
        ret_out[i] = flat(i)
        ret_copy(i, z, i).start()

    meet(z, 0, rows, True)

    half = rows // 2

    @pl.when(z == 1)
    def _():
        spread(0, lane_ids[0])
        meet(0, 0, rows, False)
        give(0)

    @pl.when(z == pivot)
    def _():
        spread(last, lane_ids[last])
        wait_chunks(last, 0, chunks)
        meet(last, 0, rows, False)
        give(last)
        spread(0, lane_ids[0])
        wait_chunks(0, 0, share)
        meet(0, 0, rows, False)
        give(0)
        spread(1, lane_ids[1])
        wait_chunks(1, 2 * share, chunks)
        meet(1, 0, rows, False)
        give(1)

    @pl.when(z == last)
    def _():
        spread(1, lane_ids[1])
        wait_chunks(1, 0, 2 * share)
        wait_chunks(1, 3 * share, chunks)
        meet(1, 0, rows, False)
        give(1)
        spread(0, lane_ids[0])
        wait_chunks(0, 0, 2 * share)
        meet(0, 0, half, False)
        wait_chunks(0, 2 * share, chunks)
        meet(0, half, rows, False)
        give(0)

    @pl.when(z > 0)
    def _():
        for b in range(subgroup):
            col_out[b] = jnp.max(col_part[:, b * rows : (b + 1) * rows], axis=0, keepdims=True)
        for k in range(1, subgroup):
            col_copy(k, s).start()

    best = flat(z)
    out_ref[...] = best.reshape(rows)

    for k in range(1, subgroup):
        level_ids_copy(k, s).wait_send()

    def sent_piece(p, carry):
        for k in range(1, others):
            level_piece(s, p, lvl_send.at[k, p], peer(2 * k)).wait_send()
            level_piece(peer(2 * k), p, fwd_send.at[k, p], partner).wait_send()
        level_piece(s, p, lvl_send.at[0, p], partner).wait_send()
        return carry

    lax.fori_loop(0, pieces, sent_piece, 0)

    def sent_chunks(copy, low, high):
        lax.fori_loop(low, high, lambda k, c: (copy(k).wait_send(), c)[1], 0)

    @pl.when(z != pivot)
    def _():
        own_ids(z).wait_send()
        sent_chunks(lambda k: own_along(k, z), 0, chunks)

    @pl.when(z == 1)
    def _():
        ids_on(0, z).wait_send()
        sent_chunks(lambda k: passed_on(0, k, z), 0, chunks)

    @pl.when(z == pivot)
    def _():
        ids_on(0, z).wait_send()
        ids_on(1, z).wait_send()
        sent_chunks(lambda k: passed_on(1, k, z), 0, 2 * share)
        sent_chunks(lambda k: passed_on(0, k, z), share, chunks)

    @pl.when(z == last)
    def _():
        sent_chunks(lambda k: passed_on(1, k, z), 2 * share, 3 * share)

    @pl.when((z > 0) & (z < last))
    def _():
        sent_chunks(lambda k: relayed(1, k), 2 * share, chunks)
        sent_chunks(lambda k: relayed(0, k), 0, share)

    @pl.when(z == 0)
    def _():
        sent_chunks(lambda k: back_across(1, k), 2 * share, 3 * share)

    @pl.when(z < pivot)
    def _():
        sent_chunks(lambda k: back_across(1, k), 3 * share, chunks)
        sent_chunks(lambda k: back_across(0, k), 0, share)

    @pl.when(z > 0)
    def _():
        out_ref[...] = jnp.maximum(out_ref[...], col_out[s].reshape(rows))
        for k in range(1, subgroup):
            col_copy(k, peer(k)).wait_recv()
            out_ref[...] = jnp.maximum(out_ref[...], col_in[peer(k)].reshape(rows))

    for j in range(1, groups):
        @pl.when((z < j) & (z < pivot) | (z > j) & (z > pivot) & (j >= pivot))
        def _(j=j):
            ret_copy(0, j, z).wait_recv()
            out_ref[...] = jnp.maximum(out_ref[...], ret_in[j].reshape(rows))

    @pl.when(z > 0)
    def _():
        for k in range(1, subgroup):
            col_copy(k, s).wait_send()
        ret_copy(0, z, 0).wait_send()

    @pl.when(z >= pivot)
    def _():
        ret_copy(1, z, 1).wait_send()

    @pl.when(z == pivot)
    def _():
        ret_copy(last, z, last).wait_send()


def by_meeting(embeddings, cluster_ids, chunks, pieces):
    rows, features = embeddings.shape
    groups = lax.axis_size("grp")
    subgroup = lax.axis_size("sub")
    dma = pltpu.SemaphoreType.DMA
    return pl.pallas_call(
        functools.partial(meet_kernel, groups, subgroup, chunks, pieces),
        out_shape=pltpu.VMEM((rows,), jnp.float32),
        in_specs=[pl.BlockSpec(memory_space=pl.ANY)] * 2,
        out_specs=pl.BlockSpec(memory_space=pltpu.VMEM),
        scratch_shapes=[
            pltpu.VMEM((rows, features), jnp.bfloat16),
            pltpu.VMEM((subgroup * rows, features), jnp.bfloat16),
            pltpu.VMEM((groups, rows, features), jnp.bfloat16),
            pltpu.VMEM((groups // 2, rows, features), jnp.bfloat16),
            pltpu.VMEM((groups, 1, rows), jnp.int32),
            pltpu.VMEM((subgroup, 1, rows), jnp.int32),
            pltpu.VMEM((groups, rows, LANES), jnp.int32),
            pltpu.VMEM((groups, rows, LANES), jnp.float32),
            pltpu.VMEM((SUBLANES, subgroup * rows), jnp.float32),
            pltpu.VMEM((groups, 1, rows), jnp.float32),
            pltpu.VMEM((groups, 1, rows), jnp.float32),
            pltpu.VMEM((subgroup, 1, rows), jnp.float32),
            pltpu.VMEM((subgroup, 1, rows), jnp.float32),
            dma((pieces,)), dma, dma((groups,)), dma((groups,)),
            dma((subgroup,)), dma((subgroup,)),
            dma((subgroup, pieces)), dma((subgroup, pieces)), dma((subgroup, pieces)),
            dma((chunks,)), dma((groups, chunks)), dma((groups, chunks)),
            dma((groups // 2, chunks)), dma((groups // 2, chunks)), dma((groups // 2, chunks)),
            dma((groups,)), dma((groups,)),
            dma((subgroup,)), dma((subgroup,)),
        ],
        compiler_params=pltpu.CompilerParams(collective_id=0, has_side_effects=True),
    )(embeddings, cluster_ids.reshape(1, rows))


def local(embeddings, cluster_ids):
    rows, features = embeddings.shape
    groups = lax.axis_size("grp")
    subgroup = lax.axis_size("sub")
    held = (groups + subgroup) * rows * features * embeddings.dtype.itemsize
    paired = lax.axis_size("rep") == 2 and subgroup % 2 == 0 and groups == 4
    if held <= VMEM_BUDGET and paired and rows % (LANES * 2) == 0:
        return by_meeting(embeddings, cluster_ids, rows // 16, 4)
    return by_owner(embeddings, cluster_ids)


def solution(mesh):
    return jax.shard_map(
        local,
        mesh=mesh,
        in_specs=(P(("rep", "grp", "sub"), None), P(("rep", "grp", "sub"), None)),
        out_specs=P(("rep", "grp", "sub")),
        check_vma=False,
    )
```

time: 37.9 us -> 36.5 us (0.963)
  the two profiles are of different devices: /device:TPU:1 before, /device:TPU:5 now
where the time goes in v1:
time: 36.5 us; the launch traced here: 36.4 us
  Pallas kernels  35.8 us (98%)
  local copies, waits for them, and re-layouts  0.56 us (2%)
    pallas_call x1, Pallas kernels, by_meeting(): pl.pallas_call(functools.partial(meet_kernel, groups, subgroup, chunks, p...  35.8 us

profile of v1, /device:TPU:5, one launch (start us, length us, event | category | flops | bytes accessed | tf_op | source)
XLA Modules:
  0.0 36.4 jit_solution(2301174171846125419)
XLA Ops:
  0.0 35.8 %shard_map.28 = f32[256]{0:T(256)S(1)} custom-call(bf16[256,1024]{1,0:T(8,128)(2,1)} %emb_ref.1, s32[1,256]{1,0:T(1,128)} %bitcast.1), custom_call_target="tpu_custom_call" | custom-call | tf_op jit(solution)/shard_map/pallas_call | solution.py:540
  35.8 0.6 %copy.4 = f32[256]{0:T(256)} copy(f32[256]{0:T(256)S(1)} %shard_map.28) | data formatting | bytes 2048

commit v2 on v1

v2 whole, which is shorter than its diff:
```python
import functools
import math

import jax
import jax.numpy as jnp
from jax import lax
from jax.experimental import pallas as pl
from jax.experimental.pallas import tpu as pltpu
from jax.sharding import PartitionSpec as P

LANES = 128
SUBLANES = 8
VMEM_BUDGET = 24 << 20
MESH = pl.DeviceIdType.MESH


def from_behind(value, axis, by):
    peers = lax.axis_size(axis)
    return lax.ppermute(value, axis, [(i, (i + by) % peers) for i in range(peers)])


def masked_maxima(left_rows, right_rows, right_present, excluded):
    similar = jnp.dot(left_rows, right_rows.T, preferred_element_type=jnp.float32)
    allowed = (right_present[None, :] > 0) & jnp.logical_not(excluded)
    return jnp.where(allowed, similar, jnp.float32(-1.0))


def unit_of(rows, features):
    floats = rows.astype(jnp.float32)
    return (
        floats
        * lax.rsqrt(jnp.mean(floats * floats, axis=1, keepdims=True) + 1e-06)
        / math.sqrt(features)
    ).astype(jnp.bfloat16)


def by_owner(embeddings, cluster_ids):
    rows_dev, features = embeddings.shape
    groups = lax.axis_size("grp")
    subgroup = lax.axis_size("sub")
    capacity = 2 * rows_dev // groups
    unit_rows = unit_of(embeddings, features)
    labels = cluster_ids[:, 0]
    member_table = (labels[:, None] == jnp.arange(groups, dtype=jnp.int32)[None, :]).astype(
        jnp.int32
    )
    running = jnp.cumsum(member_table, axis=0)
    within = jnp.sum(jnp.where(member_table > 0, running - 1, 0), axis=1)
    slot_index = labels * capacity + within
    outgoing = jnp.zeros((groups * capacity, features), jnp.bfloat16).at[slot_index].set(unit_rows)
    occupied = jnp.zeros((groups * capacity,), jnp.int32).at[slot_index].set(1)
    arrived, arrived_present = (
        lax.all_to_all(
            outgoing.reshape(groups, capacity, features),
            "grp",
            split_axis=0,
            concat_axis=0,
            tiled=True,
        ),
        lax.all_to_all(
            occupied.reshape(groups, capacity), "grp", split_axis=0, concat_axis=0, tiled=True
        ),
    )
    owned_rows = arrived.reshape(groups * capacity, features)
    present = arrived_present.reshape(groups * capacity)
    held = owned_rows.shape[0]
    positions = jnp.arange(held, dtype=jnp.int32)
    excluded = positions[:, None] == positions[None, :]
    highest = jnp.max(masked_maxima(owned_rows, owned_rows, present, excluded), axis=1)
    no_exclusion = jnp.zeros((held, held), dtype=bool)
    for offset in range(1, subgroup // 2 + 1):
        peer_rows, peer_present = from_behind((owned_rows, present), "sub", offset)
        scores = masked_maxima(owned_rows, peer_rows, peer_present, no_exclusion)
        highest = jnp.maximum(highest, jnp.max(scores, axis=1))
        if 2 * offset != subgroup:
            column_best = jnp.max(
                jnp.where(present[:, None] > 0, scores, jnp.float32(-1.0)), axis=0
            )
            returned_best = from_behind(column_best, "sub", -offset)
            highest = jnp.maximum(highest, returned_best)
    returned = lax.all_to_all(
        highest.reshape(groups, capacity), "grp", split_axis=0, concat_axis=0, tiled=True
    )
    return returned.reshape(groups * capacity)[slot_index]


LAG1 = (7, 4, 4, 4)
LAG2 = (2, 0, 4, 5, 2)


def meet_kernel(
    groups, subgroup, chunks, pieces,
    emb_ref, ids_ref, out_ref,
    emb_in, level, foreign, relay, lane_ids, level_ids, ids_col, row_part, col_part,
    ret_out, ret_in, col_out, col_in,
    in_sem, ids_in, ids_send, ids_recv, lid_recv,
    lvl_send, lvl_recv, mate_recv, own_send, pass_send, relay_send,
    first_recv, second_recv, bulk_recv, relay_recv, ret_send, ret_recv, col_recv,
):
    rows, features = emb_ref.shape
    size = rows // chunks
    load = rows // pieces
    far0 = chunks // 4
    far1 = 7 * chunks // 16
    near1 = chunks - far1
    pivot = groups // 2
    last = groups - 1
    rep = lax.axis_index("rep")
    depth = lax.axis_index("grp")
    z = depth * (1 - rep) + (last - depth) * rep
    s = lax.axis_index("sub")
    partner = s + 1 - 2 * lax.rem(s, 2)
    others = subgroup // 2
    across_y = {"rep": 1 - rep}

    def peer(k):
        return lax.rem(s + k, subgroup)

    def at(where):
        return {"grp": where * (1 - rep) + (last - where) * rep}

    def remote(src, dst, send, recv, where):
        return pltpu.make_async_remote_copy(
            src_ref=src, dst_ref=dst, send_sem=send, recv_sem=recv,
            device_id=where, device_id_type=MESH,
        )

    def slot(b):
        return pl.ds(pl.multiple_of(b * rows, rows), rows)

    def piece(b, p):
        return pl.ds(pl.multiple_of(b * rows + p * load, load), load)

    def own_chunk(k):
        return level.at[pl.ds(pl.multiple_of(s * rows + k * size, size), size), :]

    def part(k):
        return pl.ds(pl.multiple_of(k * size, size), size)

    def load_piece(p):
        where = pl.ds(pl.multiple_of(p * load, load), load)
        return pltpu.make_async_copy(emb_ref.at[where, :], emb_in.at[where, :], in_sem.at[p])

    for p in range(pieces):
        load_piece(p).start()
    ids_copy = pltpu.make_async_copy(ids_ref, level_ids.at[s], ids_in)
    ids_copy.start()

    barrier = pltpu.get_barrier_semaphore()
    for k in range(1, subgroup):
        pl.semaphore_signal(barrier, 1, device_id={"sub": peer(k)}, device_id_type=MESH)
    pl.semaphore_signal(barrier, 1, device_id=across_y, device_id_type=MESH)

    @pl.when(z > 0)
    def _():
        pl.semaphore_signal(barrier, 1, device_id=at(z - 1), device_id_type=MESH)

    @pl.when(z < last)
    def _():
        pl.semaphore_signal(barrier, 1, device_id=at(z + 1), device_id_type=MESH)

    @pl.when(z == last)
    def _():
        pl.semaphore_signal(barrier, 1, device_id=at(z - 1) | across_y, device_id_type=MESH)

    col_part[...] = jnp.full(col_part.shape, -1.0, jnp.float32)
    row_part[...] = jnp.full(row_part.shape, -1.0, jnp.float32)

    def level_ids_copy(k):
        return remote(ids_ref, level_ids.at[s], ids_send, lid_recv, {"sub": peer(k)})

    def own_ids(where):
        return remote(ids_ref, lane_ids.at[z], ids_send, ids_recv.at[z], at(where))

    def ids_on(i, where):
        return remote(lane_ids.at[i], lane_ids.at[i], ids_send, ids_recv.at[i], at(where))

    def bytes_of(count, send, recv):
        block = level.at[pl.ds(0, count), :]
        return remote(block, block, send, recv, {"sub": peer(1)})

    back0, back1, far1_recv, far0a, far0b, block3 = range(6)

    def own_along(k, where, recv):
        return remote(own_chunk(k), foreign.at[z, part(k), :], own_send, recv, at(where))

    def own_across(k):
        return remote(own_chunk(k), relay.at[1, part(k), :], own_send, relay_recv.at[k - near1], across_y)

    def passed_on(i, k, where, recv):
        block = foreign.at[i, part(k), :]
        return remote(block, block, pass_send, recv, at(where))

    def passed_across(k):
        return remote(
            foreign.at[0, part(k), :], relay.at[0, part(k), :], pass_send, relay_recv.at[far1 + k], across_y,
        )

    def relayed(i, k, j):
        block = relay.at[i, part(k), :]
        return remote(block, block, relay_send, relay_recv.at[j], at(z - 1))

    def returned(i, k, where):
        return remote(
            relay.at[i, part(k), :], foreign.at[i, part(k), :], relay_send, bulk_recv.at[back0 + i], where
        )

    def level_piece(owner, p, recv, where):
        block = level.at[piece(owner, p), :]
        return remote(block, block, lvl_send, recv, {"sub": where})

    sends_right = z < pivot
    sends_left = z == last

    def start_own(k):
        @pl.when(z == 0)
        def _():
            own_along(k, z + 1, first_recv.at[k]).start()

        @pl.when((z == 1) & (k < near1))
        def _():
            own_along(k, z + 1, second_recv.at[k]).start()

        @pl.when((z == 1) & (k >= near1))
        def _():
            own_across(k).start()

        @pl.when(sends_left)
        def _():
            own_along(k, z - 1, bulk_recv.at[block3]).start()

    step = 2 * size
    per_piece = load // step

    def normalize(h):
        where = pl.ds(pl.multiple_of(h * step, step), step)
        into = pl.ds(pl.multiple_of(s * rows + h * step, step), step)
        level[into, :] = unit_of(emb_in[where, :], features)

    def send_own(p):
        @pl.when(z != pivot)
        def _():
            lax.fori_loop(
                2 * per_piece * p, 2 * per_piece * (p + 1), lambda k, c: (start_own(k), c)[1], 0
            )

        for k in range(1, others):
            level_piece(s, p, lvl_recv.at[k, p], peer(2 * k)).start()
        level_piece(s, p, mate_recv.at[0], partner).start()

    load_piece(0).wait()
    lax.fori_loop(0, per_piece, lambda h, c: (normalize(h), c)[1], 0)
    neighbours = subgroup + sum(c.astype(jnp.int32) for c in (z > 0, z < last, z == 1))
    pl.semaphore_wait(barrier, neighbours)
    for k in range(1, subgroup):
        level_ids_copy(k).start()

    @pl.when(sends_right)
    def _():
        own_ids(z + 1).start()

    @pl.when(sends_left)
    def _():
        own_ids(z - 1).start()

    send_own(0)

    def norm_step(p, carry):
        load_piece(p).wait()
        lax.fori_loop(p * per_piece, (p + 1) * per_piece, lambda h, c: (normalize(h), c)[1], 0)
        send_own(p)
        return carry

    lax.fori_loop(1, pieces, norm_step, 0)
    ids_copy.wait()

    def level_forward(p):
        for k in range(1, others):
            arrived = level_piece(peer(subgroup - 2 * k), p, lvl_recv.at[k, p], s)
            arrived.wait_recv()
            level_piece(peer(subgroup - 2 * k), p, mate_recv.at[1], partner).start()

    def relay_step(j):
        block = 1 - jnp.minimum(j // far1, 1)
        chunk = lax.rem(j + near1, chunks)
        hold = relayed(block, chunk, j)
        hold.wait_recv()

        @pl.when(z == pivot)
        def _():
            hold.start()

        @pl.when(z == 1)
        def _():
            returned(block, chunk, across_y).start()
            returned(block, chunk, at(z - 1) | across_y).start()

    crossing = far0 + far1
    stride = chunks // pieces

    def ticks(count, native, lag_relay, lag_level):
        def tick(t, carry):
            native(t)
            j = t - lag_relay

            @pl.when((j >= 0) & (j < crossing))
            def _():
                relay_step(j)

            p = t - lag_level

            @pl.when((p >= 0) & (lax.rem(p, stride) == 0) & (p < pieces * stride))
            def _():
                level_forward(p // stride)

            return carry

        lax.fori_loop(0, count, tick, 0)

    def wait_bulk(index, count):
        bytes_of(count * size, relay_send, bulk_recv.at[index]).wait_recv()

    def spread(i, ids):
        ids_col[i] = jnp.broadcast_to(ids, (LANES, rows)).T

    def wait_home():
        bytes_of(rows, lvl_send, mate_recv.at[0]).wait_recv()
        remote(
            level_ids.at[pl.ds(0, subgroup - 1)], level_ids.at[pl.ds(0, subgroup - 1)],
            ids_send, lid_recv, {"sub": peer(1)},
        ).wait_recv()
        spread(z, level_ids[s])

    def wait_away():
        bytes_of((others - 1) * rows, lvl_send, mate_recv.at[1]).wait_recv()

    def meet(i, low, high, chip, own=False):
        count = high - low
        side = lax.rem(s // 2 + chip, others) * 2
        start = side * rows
        block = level[slot(s), :] if own else foreign[i, low:high, :]
        others_rows = level[pl.ds(pl.multiple_of(start, 2 * rows), 2 * rows), :]
        similar = lax.dot_general(
            block, others_rows, (((1,), (1,)), ((), ())), preferred_element_type=jnp.float32
        )
        own_ids = ids_col[i, low:high, :]
        best = row_part[i, low:high, :]
        for col in range(0, 2 * rows, LANES):
            same = own_ids == level_ids[side + col // rows, :, col % rows : col % rows + LANES]
            if own:
                across = lax.broadcasted_iota(jnp.int32, (rows, LANES), 1) + (col + start)
                down = lax.broadcasted_iota(jnp.int32, (rows, LANES), 0) + s * rows
                same = same & (across != down)
            kept = jnp.where(same, similar[:, col : col + LANES], jnp.float32(-1.0))
            best = jnp.maximum(best, kept)
            if not own:
                columns = jnp.max(kept.reshape(count // SUBLANES, SUBLANES, LANES), axis=0)
                where = pl.ds(pl.multiple_of(start + col, LANES), LANES)
                col_part[:, where] = jnp.maximum(col_part[:, where], columns)
        row_part[i, low:high, :] = best

    def meet_all(i, low, high, own=False):
        for chip in range(others):
            meet(i, low, high, chip, own)

    def flat(i):
        return jnp.max(row_part[i].T, axis=0, keepdims=True)

    def ret_copy(i, owner, where):
        return remote(ret_out.at[i], ret_in.at[owner], ret_send, ret_recv.at[owner], at(where))

    def col_copy(k):
        return remote(col_out.at[peer(k)], col_in.at[s], ret_send, col_recv, {"sub": peer(k)})

    def give(i):
        ret_out[i] = flat(i)
        ret_copy(i, z, i).start()

    half = rows // 2

    @pl.when((z == 0) | (z == last))
    def _():
        lax.fori_loop(0, pieces, lambda p, c: (level_forward(p), c)[1], 0)
        wait_home()
        wait_away()
        meet_all(z, 0, rows, True)

    @pl.when(z == 1)
    def _():
        ids_on(0, z).wait_recv()
        ids_on(0, z + 1).start()

        def native(k):
            @pl.when(k < chunks)
            def _():
                passed_on(0, k, z, first_recv.at[k]).wait_recv()

                @pl.when(k < far0)
                def _():
                    passed_across(k).start()

                @pl.when(k >= far0)
                def _():
                    passed_on(0, k, z + 1, first_recv.at[k]).start()

        ticks(
            max(LAG1[0] + crossing, LAG1[2] + chunks), native,
            LAG1[0] * (1 - rep) + LAG1[1] * rep, LAG1[2] * (1 - rep) + LAG1[3] * rep,
        )
        wait_home()
        wait_away()
        meet_all(z, 0, rows, True)
        spread(0, lane_ids[0])
        meet_all(0, 0, rows)
        give(0)

    @pl.when(z == pivot)
    def _():
        ids_on(1, z).wait_recv()
        ids_on(1, z + 1).start()
        lead = LAG2[4]
        steps = near1 + chunks - far0

        def native(t):
            k = t - lead * rep

            @pl.when((k >= 0) & (k < near1))
            def _():
                passed_on(1, k, z, second_recv.at[k]).wait_recv()
                passed_on(1, k, z + 1, bulk_recv.at[far1_recv]).start()

            m = k - near1 + far0

            @pl.when(k == near1)
            def _():
                ids_on(0, z).wait_recv()
                ids_on(0, z + 1).start()

            @pl.when((k >= near1) & (m < chunks))
            def _():
                passed_on(0, m, z, first_recv.at[m]).wait_recv()

            @pl.when((k >= near1) & (m < chunks // 2))
            def _():
                passed_on(0, m, z + 1, bulk_recv.at[far0a]).start()

            @pl.when((k >= near1) & (m >= chunks // 2) & (m < chunks))
            def _():
                passed_on(0, m, z + 1, bulk_recv.at[far0b]).start()

            @pl.when(k == steps - 9)
            def _():
                wait_home()
                meet(z, 0, rows, 0, True)

            @pl.when(k == steps - 7)
            def _():
                spread(1, lane_ids[1])
                meet(1, 0, half, 0)

            @pl.when(k == steps - 3)
            def _():
                ids_on(last, z).wait_recv()
                spread(last, lane_ids[last])
                wait_bulk(block3, chunks)
                meet(last, 0, rows, 0)

            @pl.when(k == steps - 2)
            def _():
                wait_away()
                for chip in range(1, others):
                    meet(z, 0, rows, chip, True)

            @pl.when(k == steps - 1)
            def _():
                for chip in range(1, others):
                    meet(last, 0, rows, chip)

        ticks(
            steps + lead, native,
            LAG2[0] * (1 - rep) + LAG2[1] * rep, LAG2[2] * (1 - rep) + LAG2[3] * rep,
        )
        spread(0, lane_ids[0])
        wait_bulk(back0, far0)
        meet_all(0, 0, rows)
        give(0)
        wait_bulk(back1, far1)
        for chip in range(1, others):
            meet(1, 0, half, chip)
        meet_all(1, half, rows)
        give(1)
        give(last)

    @pl.when(z == last)
    def _():
        ids_on(1, z).wait_recv()
        spread(1, lane_ids[1])
        ids_on(0, z).wait_recv()
        spread(0, lane_ids[0])
        wait_bulk(far1_recv, near1)
        meet_all(1, 0, half)
        wait_bulk(back1, far1)
        meet_all(1, half, rows)
        give(1)
        wait_bulk(back0, far0)
        wait_bulk(far0a, chunks // 2 - far0)
        meet_all(0, 0, half)
        wait_bulk(far0b, chunks // 2)
        meet_all(0, half, rows)
        give(0)

    @pl.when(z > 0)
    def _():
        for b in range(subgroup):
            col_out[b] = jnp.max(col_part[:, b * rows : (b + 1) * rows], axis=0, keepdims=True)
        for k in range(1, subgroup):
            col_copy(k).start()

    out_ref[...] = flat(z).reshape(rows)

    bytes_of(2 * (others - 1) * rows + rows, lvl_send, col_recv).wait_send()

    def sent_ids(count):
        block = lane_ids.at[pl.ds(0, count)]
        remote(block, block, ids_send, col_recv, {"sub": peer(1)}).wait_send()

    @pl.when((z == 0) | (z == last))
    def _():
        sent_ids(subgroup)

    @pl.when((z > 0) & (z < last))
    def _():
        sent_ids(subgroup + 1)

    @pl.when(z != pivot)
    def _():
        bytes_of(rows, own_send, col_recv).wait_send()

    @pl.when(z == 1)
    def _():
        bytes_of(rows, pass_send, col_recv).wait_send()
        bytes_of(2 * crossing * size, relay_send, col_recv).wait_send()

    @pl.when(z == pivot)
    def _():
        bytes_of((near1 + chunks - far0) * size, pass_send, col_recv).wait_send()
        bytes_of(crossing * size, relay_send, col_recv).wait_send()

    @pl.when(z > 0)
    def _():
        block = col_in.at[pl.ds(0, subgroup - 1)]
        remote(block, block, ret_send, col_recv, {"sub": peer(1)}).wait_recv()
        heard = col_out[s]
        for k in range(1, subgroup):
            heard = jnp.maximum(heard, col_in[peer(k)])
        out_ref[...] = jnp.maximum(out_ref[...], heard.reshape(rows))

    for j in range(1, groups):
        @pl.when((z < j) & (z < pivot) | (z > j) & (z > pivot) & (j >= pivot))
        def _(j=j):
            ret_copy(0, j, z).wait_recv()
            out_ref[...] = jnp.maximum(out_ref[...], ret_in[j].reshape(rows))

    def sent_maxima(count):
        block = col_in.at[pl.ds(0, count)]
        remote(block, block, ret_send, col_recv, {"sub": peer(1)}).wait_send()

    for here, count in ((1, 1), (pivot, 3), (last, 2)):
        @pl.when(z == here)
        def _(count=count):
            sent_maxima(subgroup - 1 + count)


def by_meeting(embeddings, cluster_ids, chunks, pieces):
    rows, features = embeddings.shape
    groups = lax.axis_size("grp")
    subgroup = lax.axis_size("sub")
    dma = pltpu.SemaphoreType.DMA
    return pl.pallas_call(
        functools.partial(meet_kernel, groups, subgroup, chunks, pieces),
        out_shape=pltpu.VMEM((rows,), jnp.float32),
        in_specs=[pl.BlockSpec(memory_space=pl.ANY)] * 2,
        out_specs=pl.BlockSpec(memory_space=pltpu.VMEM),
        scratch_shapes=[
            pltpu.VMEM((rows, features), jnp.bfloat16),
            pltpu.VMEM((subgroup * rows, features), jnp.bfloat16),
            pltpu.VMEM((groups, rows, features), jnp.bfloat16),
            pltpu.VMEM((groups // 2, rows, features), jnp.bfloat16),
            pltpu.VMEM((2 * subgroup, 1, rows), jnp.int32),
            pltpu.VMEM((subgroup, 1, rows), jnp.int32),
            pltpu.VMEM((groups, rows, LANES), jnp.int32),
            pltpu.VMEM((groups, rows, LANES), jnp.float32),
            pltpu.VMEM((SUBLANES, subgroup * rows), jnp.float32),
            pltpu.VMEM((groups, 1, rows), jnp.float32),
            pltpu.VMEM((groups, 1, rows), jnp.float32),
            pltpu.VMEM((subgroup, 1, rows), jnp.float32),
            pltpu.VMEM((2 * subgroup, 1, rows), jnp.float32),
            dma((pieces,)), dma, dma, dma((groups,)), dma,
            dma, dma((subgroup // 2, pieces)), dma((2,)), dma, dma, dma,
            dma((chunks,)), dma((chunks,)), dma((6,)), dma((chunks,)), dma, dma((groups,)), dma,
        ],
        compiler_params=pltpu.CompilerParams(collective_id=0, has_side_effects=True),
    )(embeddings, cluster_ids.reshape(1, rows))


def local(embeddings, cluster_ids):
    rows, features = embeddings.shape
    groups = lax.axis_size("grp")
    subgroup = lax.axis_size("sub")
    held = (groups + subgroup) * rows * features * embeddings.dtype.itemsize
    paired = lax.axis_size("rep") == 2 and subgroup % 2 == 0 and groups == 4
    if held <= VMEM_BUDGET and paired and rows % (LANES * 2) == 0:
        return by_meeting(embeddings, cluster_ids, rows // 16, 4)
    return by_owner(embeddings, cluster_ids)


def solution(mesh):
    return jax.shard_map(
        local,
        mesh=mesh,
        in_specs=(P(("rep", "grp", "sub"), None), P(("rep", "grp", "sub"), None)),
        out_specs=P(("rep", "grp", "sub")),
        check_vma=False,
    )
```

time: 36.5 us -> 29.9 us (0.82)
  the two profiles are of different devices: /device:TPU:5 before, /device:TPU:0 now
where the time goes in v2:
time: 29.9 us; the launch traced here: 29.7 us
  Pallas kernels  29.2 us (98%)
  local copies, waits for them, and re-layouts  0.56 us (2%)
    pallas_call x1, Pallas kernels, by_meeting(): pl.pallas_call(functools.partial(meet_kernel, groups, subgroup, chunks, p...  29.2 us

profile of v2, /device:TPU:0, one launch (start us, length us, event | category | flops | bytes accessed | tf_op | source)
XLA Modules:
  0.0 29.7 jit_solution(15077554937203159621)
XLA Ops:
  0.0 29.2 %shard_map.28 = f32[256]{0:T(256)S(1)} custom-call(bf16[256,1024]{1,0:T(8,128)(2,1)} %emb_ref.1, s32[1,256]{1,0:T(1,128)} %bitcast.1), custom_call_target="tpu_custom_call" | custom-call | tf_op jit(solution)/shard_map/pallas_call | solution.py:579
  29.2 0.6 %copy.4 = f32[256]{0:T(256)} copy(f32[256]{0:T(256)S(1)} %shard_map.28) | data formatting | bytes 2048

commit v3 on v2

--- a/solution.py
+++ b/solution.py
@@ -85,7 +85,10 @@
 
 
 LAG1 = (7, 4, 4, 4)
-LAG2 = (2, 0, 4, 5, 2)
+LAG2 = (2, 0, 4, 4, 2)
+LEAD = (5, 6)
+FAR1 = (7, 9)
+EARLY1 = 6
 
 
 def meet_kernel(
@@ -101,14 +104,19 @@
     size = rows // chunks
     load = rows // pieces
     far0 = chunks // 4
-    far1 = 7 * chunks // 16
-    near1 = chunks - far1
+    near0 = chunks - far0
+    unit = chunks // 16
+    early1 = EARLY1 * unit
     pivot = groups // 2
     last = groups - 1
     rep = lax.axis_index("rep")
     depth = lax.axis_index("grp")
     z = depth * (1 - rep) + (last - depth) * rep
     s = lax.axis_index("sub")
+    far1 = unit * (FAR1[0] * (1 - rep) + FAR1[1] * rep)
+    near1 = chunks - far1
+    their_far1 = unit * (FAR1[1] * (1 - rep) + FAR1[0] * rep)
+    their_near1 = chunks - their_far1
     partner = s + 1 - 2 * lax.rem(s, 2)
     others = subgroup // 2
     across_y = {"rep": 1 - rep}
@@ -141,8 +149,13 @@
         where = pl.ds(pl.multiple_of(p * load, load), load)
         return pltpu.make_async_copy(emb_ref.at[where, :], emb_in.at[where, :], in_sem.at[p])
 
+    turn = jnp.where(z == 0, pieces - 1, 0)
+
+    def turned(p):
+        return lax.rem(p + turn, pieces)
+
     for p in range(pieces):
-        load_piece(p).start()
+        load_piece(turned(p)).start()
     ids_copy = pltpu.make_async_copy(ids_ref, level_ids.at[s], ids_in)
     ids_copy.start()
 
@@ -179,23 +192,20 @@
         block = level.at[pl.ds(0, count), :]
         return remote(block, block, send, recv, {"sub": peer(1)})
 
-    back0, back1, far1_recv, far0a, far0b, block3 = range(6)
+    back0, back1, far1_recv, far0a, far0b, block3, rest0 = range(7)
+    ahead = 3 * chunks // 8
+    lead1 = unit * (LEAD[0] * (1 - rep) + LEAD[1] * rep)
 
     def own_along(k, where, recv):
         return remote(own_chunk(k), foreign.at[z, part(k), :], own_send, recv, at(where))
 
-    def own_across(k):
-        return remote(own_chunk(k), relay.at[1, part(k), :], own_send, relay_recv.at[k - near1], across_y)
+    def own_across(i, k, j):
+        return remote(own_chunk(k), relay.at[i, part(k), :], own_send, relay_recv.at[j], across_y)
 
     def passed_on(i, k, where, recv):
         block = foreign.at[i, part(k), :]
         return remote(block, block, pass_send, recv, at(where))
 
-    def passed_across(k):
-        return remote(
-            foreign.at[0, part(k), :], relay.at[0, part(k), :], pass_send, relay_recv.at[far1 + k], across_y,
-        )
-
     def relayed(i, k, j):
         block = relay.at[i, part(k), :]
         return remote(block, block, relay_send, relay_recv.at[j], at(z - 1))
@@ -213,24 +223,29 @@
     sends_left = z == last
 
     def start_own(k):
-        @pl.when(z == 0)
+        @pl.when((z == 0) & (k < near0))
         def _():
             own_along(k, z + 1, first_recv.at[k]).start()
 
-        @pl.when((z == 1) & (k < near1))
+        @pl.when((z == 0) & (k >= near0))
+        def _():
+            own_across(0, k, early1 + k - near0).start()
+
+        @pl.when((z == 1) & (k < lead1))
         def _():
             own_along(k, z + 1, second_recv.at[k]).start()
 
         @pl.when((z == 1) & (k >= near1))
         def _():
-            own_across(k).start()
-
-        @pl.when(sends_left)
+            own_across(1, k, k - near1 + jnp.where(k < near1 + early1, 0, far0)).start()
+
+        @pl.when((z == last) & (k < ahead))
         def _():
             own_along(k, z - 1, bulk_recv.at[block3]).start()
 
-    step = 2 * size
+    step = rows // 8
     per_piece = load // step
+    per_load = load // size
 
     def normalize(h):
         where = pl.ds(pl.multiple_of(h * step, step), step)
@@ -241,15 +256,17 @@
         @pl.when(z != pivot)
         def _():
             lax.fori_loop(
-                2 * per_piece * p, 2 * per_piece * (p + 1), lambda k, c: (start_own(k), c)[1], 0
+                per_load * p, per_load * (p + 1), lambda k, c: (start_own(k), c)[1], 0
             )
 
         for k in range(1, others):
-            level_piece(s, p, lvl_recv.at[k, p], peer(2 * k)).start()
+            level_piece(s, p, lvl_recv.at[k - 1, p], peer(2 * k)).start()
         level_piece(s, p, mate_recv.at[0], partner).start()
 
-    load_piece(0).wait()
-    lax.fori_loop(0, per_piece, lambda h, c: (normalize(h), c)[1], 0)
+    load_piece(turn).wait()
+    lax.fori_loop(
+        turn * per_piece, (turn + 1) * per_piece, lambda h, c: (normalize(h), c)[1], 0
+    )
     neighbours = subgroup + sum(c.astype(jnp.int32) for c in (z > 0, z < last, z == 1))
     pl.semaphore_wait(barrier, neighbours)
     for k in range(1, subgroup):
@@ -263,9 +280,10 @@
     def _():
         own_ids(z - 1).start()
 
-    send_own(0)
-
-    def norm_step(p, carry):
+    send_own(turn)
+
+    def norm_step(q, carry):
+        p = turned(q)
         load_piece(p).wait()
         lax.fori_loop(p * per_piece, (p + 1) * per_piece, lambda h, c: (normalize(h), c)[1], 0)
         send_own(p)
@@ -276,17 +294,19 @@
 
     def level_forward(p):
         for k in range(1, others):
-            arrived = level_piece(peer(subgroup - 2 * k), p, lvl_recv.at[k, p], s)
+            arrived = level_piece(peer(subgroup - 2 * k), p, lvl_recv.at[k - 1, p], s)
             arrived.wait_recv()
             level_piece(peer(subgroup - 2 * k), p, mate_recv.at[1], partner).start()
 
     def relay_step(j):
-        block = 1 - jnp.minimum(j // far1, 1)
-        chunk = lax.rem(j + near1, chunks)
+        block = jnp.where((j < early1) | (j >= early1 + far0), 1, 0)
+        chunk = j + jnp.where(
+            j < early1, their_near1, jnp.where(j < early1 + far0, near0 - early1, their_near1 - far0)
+        )
         hold = relayed(block, chunk, j)
         hold.wait_recv()
 
-        @pl.when(z == pivot)
+        @pl.when(z >= pivot)
         def _():
             hold.start()
 
@@ -295,7 +315,7 @@
             returned(block, chunk, across_y).start()
             returned(block, chunk, at(z - 1) | across_y).start()
 
-    crossing = far0 + far1
+    crossing = far0 + their_far1
     stride = chunks // pieces
 
     def ticks(count, native, lag_relay, lag_level):
@@ -316,6 +336,12 @@
             return carry
 
         lax.fori_loop(0, count, tick, 0)
+
+    def either_way(body):
+        for way, far in enumerate(FAR1):
+            @pl.when(rep == way)
+            def _(far=far):
+                body(far * unit)
 
     def wait_bulk(index, count):
         bytes_of(count * size, relay_send, bulk_recv.at[index]).wait_recv()
@@ -378,39 +404,66 @@
 
     half = rows // 2
 
+    @pl.when(z == 0)
+    def _():
+        lax.fori_loop(
+            near0, chunks, lambda k, c: (own_along(k, z + 1, bulk_recv.at[rest0]).start(), c)[1], 0
+        )
+
+    @pl.when(z == last)
+    def _():
+        lax.fori_loop(
+            early1, early1 + far0, lambda j, c: (relay_step(j), c)[1], 0
+        )
+        lax.fori_loop(
+            ahead, chunks, lambda k, c: (own_along(k, z - 1, bulk_recv.at[block3]).start(), c)[1], 0
+        )
+
     @pl.when((z == 0) | (z == last))
     def _():
-        lax.fori_loop(0, pieces, lambda p, c: (level_forward(p), c)[1], 0)
-        wait_home()
+        def early(p, carry):
+            level_forward(p)
+
+            @pl.when(p == pieces // 2)
+            def _():
+                wait_home()
+                meet(z, 0, rows, 0, True)
+
+            return carry
+
+        lax.fori_loop(0, pieces, early, 0)
         wait_away()
-        meet_all(z, 0, rows, True)
+        for chip in range(1, others):
+            meet(z, 0, rows, chip, True)
 
     @pl.when(z == 1)
     def _():
         ids_on(0, z).wait_recv()
         ids_on(0, z + 1).start()
 
-        def native(k):
-            @pl.when(k < chunks)
-            def _():
-                passed_on(0, k, z, first_recv.at[k]).wait_recv()
-
-                @pl.when(k < far0)
-                def _():
-                    passed_across(k).start()
-
-                @pl.when(k >= far0)
-                def _():
-                    passed_on(0, k, z + 1, first_recv.at[k]).start()
+        def native(t):
+            @pl.when(t < near0)
+            def _():
+                passed_on(0, t, z, first_recv.at[t]).wait_recv()
+                passed_on(0, t, z + 1, first_recv.at[t]).start()
+
+            @pl.when(t == near0 - 1)
+            def _():
+                lax.fori_loop(
+                    lead1, near1,
+                    lambda k, c: (own_along(k, z + 1, second_recv.at[k]).start(), c)[1], 0,
+                )
 
         ticks(
-            max(LAG1[0] + crossing, LAG1[2] + chunks), native,
-            LAG1[0] * (1 - rep) + LAG1[1] * rep, LAG1[2] * (1 - rep) + LAG1[3] * rep,
+            max(LAG1[0] * unit + far0 + max(FAR1) * unit, (LAG1[2] + 12) * unit + 1), native,
+            unit * (LAG1[0] * (1 - rep) + LAG1[1] * rep),
+            unit * (LAG1[2] * (1 - rep) + LAG1[3] * rep),
         )
         wait_home()
         wait_away()
         meet_all(z, 0, rows, True)
         spread(0, lane_ids[0])
+        wait_bulk(rest0, far0)
         meet_all(0, 0, rows)
         give(0)
 
@@ -418,96 +471,83 @@
     def _():
         ids_on(1, z).wait_recv()
         ids_on(1, z + 1).start()
-        lead = LAG2[4]
-        steps = near1 + chunks - far0
+        lead = LAG2[4] * unit
+        steps = near1 + near0
 
         def native(t):
             k = t - lead * rep
 
-            @pl.when((k >= 0) & (k < near1))
-            def _():
-                passed_on(1, k, z, second_recv.at[k]).wait_recv()
-                passed_on(1, k, z + 1, bulk_recv.at[far1_recv]).start()
-
-            m = k - near1 + far0
-
-            @pl.when(k == near1)
+            m = k - lead1
+            own = k - jnp.where(k < lead1, 0, near0)
+
+            @pl.when((k >= 0) & (k < lead1) | (k >= lead1 + near0) & (k < steps))
+            def _():
+                passed_on(1, own, z, second_recv.at[own]).wait_recv()
+                passed_on(1, own, z + 1, bulk_recv.at[far1_recv]).start()
+
+            @pl.when(m == 0)
             def _():
                 ids_on(0, z).wait_recv()
                 ids_on(0, z + 1).start()
 
-            @pl.when((k >= near1) & (m < chunks))
+            @pl.when((m >= 0) & (m < near0))
             def _():
                 passed_on(0, m, z, first_recv.at[m]).wait_recv()
 
-            @pl.when((k >= near1) & (m < chunks // 2))
+            @pl.when((m >= 0) & (m < chunks // 2))
             def _():
                 passed_on(0, m, z + 1, bulk_recv.at[far0a]).start()
 
-            @pl.when((k >= near1) & (m >= chunks // 2) & (m < chunks))
+            @pl.when((m >= chunks // 2) & (m < near0))
             def _():
                 passed_on(0, m, z + 1, bulk_recv.at[far0b]).start()
 
-            @pl.when(k == steps - 9)
+            @pl.when(k == steps - 9 * unit)
             def _():
                 wait_home()
                 meet(z, 0, rows, 0, True)
 
-            @pl.when(k == steps - 7)
-            def _():
-                spread(1, lane_ids[1])
-                meet(1, 0, half, 0)
-
-            @pl.when(k == steps - 3)
-            def _():
-                ids_on(last, z).wait_recv()
-                spread(last, lane_ids[last])
-                wait_bulk(block3, chunks)
-                meet(last, 0, rows, 0)
-
-            @pl.when(k == steps - 2)
+            @pl.when(k == steps - 2 * unit)
             def _():
                 wait_away()
                 for chip in range(1, others):
                     meet(z, 0, rows, chip, True)
 
-            @pl.when(k == steps - 1)
-            def _():
-                for chip in range(1, others):
-                    meet(last, 0, rows, chip)
-
         ticks(
             steps + lead, native,
-            LAG2[0] * (1 - rep) + LAG2[1] * rep, LAG2[2] * (1 - rep) + LAG2[3] * rep,
+            unit * (LAG2[0] * (1 - rep) + LAG2[1] * rep),
+            unit * (LAG2[2] * (1 - rep) + LAG2[3] * rep),
         )
         spread(0, lane_ids[0])
         wait_bulk(back0, far0)
         meet_all(0, 0, rows)
         give(0)
-        wait_bulk(back1, far1)
-        for chip in range(1, others):
-            meet(1, 0, half, chip)
-        meet_all(1, half, rows)
+        spread(1, lane_ids[1])
+        either_way(lambda far: wait_bulk(back1, far))
+        meet_all(1, 0, rows)
         give(1)
+        ids_on(last, z).wait_recv()
+        spread(last, lane_ids[last])
+        wait_bulk(block3, chunks)
+        meet_all(last, 0, rows)
         give(last)
 
     @pl.when(z == last)
     def _():
+        ids_on(0, z).wait_recv()
+        spread(0, lane_ids[0])
         ids_on(1, z).wait_recv()
         spread(1, lane_ids[1])
-        ids_on(0, z).wait_recv()
-        spread(0, lane_ids[0])
-        wait_bulk(far1_recv, near1)
-        meet_all(1, 0, half)
-        wait_bulk(back1, far1)
-        meet_all(1, half, rows)
-        give(1)
+        wait_bulk(far0a, chunks // 2)
+        meet_all(0, 0, half)
+        wait_bulk(far0b, near0 - chunks // 2)
         wait_bulk(back0, far0)
-        wait_bulk(far0a, chunks // 2 - far0)
-        meet_all(0, 0, half)
-        wait_bulk(far0b, chunks // 2)
         meet_all(0, half, rows)
         give(0)
+        either_way(lambda far: wait_bulk(back1, far))
+        either_way(lambda far: wait_bulk(far1_recv, chunks - far))
+        meet_all(1, 0, rows)
+        give(1)
 
     @pl.when(z > 0)
     def _():
@@ -532,19 +572,37 @@
     def _():
         sent_ids(subgroup + 1)
 
-    @pl.when(z != pivot)
+    @pl.when(z == 0)
+    def _():
+        bytes_of((chunks + far0) * size, own_send, col_recv).wait_send()
+
+    @pl.when((z == 1) | (z == last))
     def _():
         bytes_of(rows, own_send, col_recv).wait_send()
 
+    @pl.when(z == last)
+    def _():
+        bytes_of(far0 * size, relay_send, col_recv).wait_send()
+
     @pl.when(z == 1)
     def _():
-        bytes_of(rows, pass_send, col_recv).wait_send()
-        bytes_of(2 * crossing * size, relay_send, col_recv).wait_send()
+        bytes_of((chunks - far0) * size, pass_send, col_recv).wait_send()
+        either_way(
+            lambda far: bytes_of(
+                2 * (far0 + sum(FAR1) * unit - far) * size, relay_send, col_recv
+            ).wait_send()
+        )
 
     @pl.when(z == pivot)
     def _():
-        bytes_of((near1 + chunks - far0) * size, pass_send, col_recv).wait_send()
-        bytes_of(crossing * size, relay_send, col_recv).wait_send()
+        either_way(
+            lambda far: bytes_of((chunks - far + near0) * size, pass_send, col_recv).wait_send()
+        )
+        either_way(
+            lambda far: bytes_of(
+                (far0 + sum(FAR1) * unit - far) * size, relay_send, col_recv
+            ).wait_send()
+        )
 
     @pl.when(z > 0)
     def _():
@@ -596,8 +654,10 @@
             pltpu.VMEM((subgroup, 1, rows), jnp.float32),
             pltpu.VMEM((2 * subgroup, 1, rows), jnp.float32),
             dma((pieces,)), dma, dma, dma((groups,)), dma,
-            dma, dma((subgroup // 2, pieces)), dma((2,)), dma, dma, dma,
-            dma((chunks,)), dma((chunks,)), dma((6,)), dma((chunks,)), dma, dma((groups,)), dma,
+            dma, dma((max(subgroup // 2 - 1, 1), pieces)), dma((2,)), dma, dma, dma,
+            dma((3 * chunks // 4,)), dma((chunks - min(FAR1) * chunks // 16,)), dma((7,)),
+            dma((chunks // 4 + max(FAR1) * chunks // 16,)),
+            dma, dma((groups,)), dma,
         ],
         compiler_params=pltpu.CompilerParams(collective_id=0, has_side_effects=True),
     )(embeddings, cluster_ids.reshape(1, rows))

time: 29.9 us -> 27.2 us (0.910)
  Pallas kernels: 29.2 us -> 26.5 us
    pallas_call x1, Pallas kernels: 29.2 us -> 26.5 us  [by_meeting(): pl.pallas_call(functools.partial(meet_kernel, groups, subgroup, chunks, p...]
where the time goes in v3:
time: 27.2 us; the launch traced here: 27 us
  Pallas kernels  26.5 us (97%)
  local copies, waits for them, and re-layouts  0.56 us (2%)
    pallas_call x1, Pallas kernels, by_meeting(): pl.pallas_call(functools.partial(meet_kernel, groups, subgroup, chunks, p...  26.5 us
    unnamed x1, local copies, waits for them, and re-layouts  0.56 us

profile of v3, /device:TPU:0, one launch (start us, length us, event | category | flops | bytes accessed | tf_op | source)
XLA Modules:
  0.0 27.0 jit_solution(11972989564437848039)
XLA Ops:
  0.0 26.5 %shard_map.28 = f32[256]{0:T(256)S(1)} custom-call(bf16[256,1024]{1,0:T(8,128)(2,1)} %emb_ref.1, s32[1,256]{1,0:T(1,128)} %bitcast.1), custom_call_target="tpu_custom_call" | custom-call | tf_op jit(solution)/shard_map/pallas_call | solution.py:637
  26.5 0.6 %copy.4 = f32[256]{0:T(256)} copy(f32[256]{0:T(256)S(1)} %shard_map.28) | data formatting | bytes 2048

commit v4 on v3

--- a/solution.py
+++ b/solution.py
@@ -85,10 +85,14 @@
 
 
 LAG1 = (7, 4, 4, 4)
-LAG2 = (2, 0, 4, 4, 2)
-LEAD = (5, 6)
+LAG2 = (1, 0, 4, 4, 2)
+REST0 = 1
+HOME = (5, 9)
+LEAD = (3, 7)
 FAR1 = (7, 9)
-EARLY1 = 6
+EARLY1 = (4, 6)
+AHEAD = (6, 4)
+SKIP = 1
 
 
 def meet_kernel(
@@ -106,7 +110,7 @@
     far0 = chunks // 4
     near0 = chunks - far0
     unit = chunks // 16
-    early1 = EARLY1 * unit
+    skip = SKIP * unit
     pivot = groups // 2
     last = groups - 1
     rep = lax.axis_index("rep")
@@ -117,6 +121,8 @@
     near1 = chunks - far1
     their_far1 = unit * (FAR1[1] * (1 - rep) + FAR1[0] * rep)
     their_near1 = chunks - their_far1
+    early1 = unit * (EARLY1[0] * (1 - rep) + EARLY1[1] * rep)
+    their_early1 = unit * (EARLY1[1] * (1 - rep) + EARLY1[0] * rep)
     partner = s + 1 - 2 * lax.rem(s, 2)
     others = subgroup // 2
     across_y = {"rep": 1 - rep}
@@ -192,8 +198,9 @@
         block = level.at[pl.ds(0, count), :]
         return remote(block, block, send, recv, {"sub": peer(1)})
 
-    back0, back1, far1_recv, far0a, far0b, block3, rest0 = range(7)
-    ahead = 3 * chunks // 8
+    back0, back1, block3 = range(3)
+    far1_recv, far0a, far0b, rest0 = range(4)
+    ahead = unit * (AHEAD[0] * (1 - rep) + AHEAD[1] * rep)
     lead1 = unit * (LEAD[0] * (1 - rep) + LEAD[1] * rep)
 
     def own_along(k, where, recv):
@@ -299,9 +306,9 @@
             level_piece(peer(subgroup - 2 * k), p, mate_recv.at[1], partner).start()
 
     def relay_step(j):
-        block = jnp.where((j < early1) | (j >= early1 + far0), 1, 0)
+        block = jnp.where((j < their_early1) | (j >= their_early1 + far0), 1, 0)
         chunk = j + jnp.where(
-            j < early1, their_near1, jnp.where(j < early1 + far0, near0 - early1, their_near1 - far0)
+            j < their_early1, their_near1, jnp.where(j < their_early1 + far0, near0 - their_early1, their_near1 - far0)
         )
         hold = relayed(block, chunk, j)
         hold.wait_recv()
@@ -343,8 +350,8 @@
             def _(far=far):
                 body(far * unit)
 
-    def wait_bulk(index, count):
-        bytes_of(count * size, relay_send, bulk_recv.at[index]).wait_recv()
+    def wait_bulk(index, count, among=bulk_recv):
+        bytes_of(count * size, relay_send, among.at[index]).wait_recv()
 
     def spread(i, ids):
         ids_col[i] = jnp.broadcast_to(ids, (LANES, rows)).T
@@ -361,29 +368,40 @@
         bytes_of((others - 1) * rows, lvl_send, mate_recv.at[1]).wait_recv()
 
     def meet(i, low, high, chip, own=False):
-        count = high - low
+        meet_rows(((i, low, high),), chip, own)
+
+    def meet_rows(parts, chip, own=False):
         side = lax.rem(s // 2 + chip, others) * 2
         start = side * rows
-        block = level[slot(s), :] if own else foreign[i, low:high, :]
+        if own:
+            block = level[slot(s), :]
+        else:
+            block = jnp.concatenate([foreign[i, low:high, :] for i, low, high in parts], axis=0)
         others_rows = level[pl.ds(pl.multiple_of(start, 2 * rows), 2 * rows), :]
         similar = lax.dot_general(
             block, others_rows, (((1,), (1,)), ((), ())), preferred_element_type=jnp.float32
         )
-        own_ids = ids_col[i, low:high, :]
-        best = row_part[i, low:high, :]
-        for col in range(0, 2 * rows, LANES):
-            same = own_ids == level_ids[side + col // rows, :, col % rows : col % rows + LANES]
-            if own:
-                across = lax.broadcasted_iota(jnp.int32, (rows, LANES), 1) + (col + start)
-                down = lax.broadcasted_iota(jnp.int32, (rows, LANES), 0) + s * rows
-                same = same & (across != down)
-            kept = jnp.where(same, similar[:, col : col + LANES], jnp.float32(-1.0))
-            best = jnp.maximum(best, kept)
-            if not own:
-                columns = jnp.max(kept.reshape(count // SUBLANES, SUBLANES, LANES), axis=0)
-                where = pl.ds(pl.multiple_of(start + col, LANES), LANES)
-                col_part[:, where] = jnp.maximum(col_part[:, where], columns)
-        row_part[i, low:high, :] = best
+        top = 0
+        for i, low, high in parts:
+            count = high - low
+            own_ids = ids_col[i, low:high, :]
+            best = row_part[i, low:high, :]
+            for col in range(0, 2 * rows, LANES):
+                same = own_ids == level_ids[side + col // rows, :, col % rows : col % rows + LANES]
+                if own:
+                    across = lax.broadcasted_iota(jnp.int32, (rows, LANES), 1) + (col + start)
+                    down = lax.broadcasted_iota(jnp.int32, (rows, LANES), 0) + s * rows
+                    same = same & (across != down)
+                kept = jnp.where(
+                    same, similar[top : top + count, col : col + LANES], jnp.float32(-1.0)
+                )
+                best = jnp.maximum(best, kept)
+                if not own:
+                    columns = jnp.max(kept.reshape(count // SUBLANES, SUBLANES, LANES), axis=0)
+                    where = pl.ds(pl.multiple_of(start + col, LANES), LANES)
+                    col_part[:, where] = jnp.maximum(col_part[:, where], columns)
+            row_part[i, low:high, :] = best
+            top += count
 
     def meet_all(i, low, high, own=False):
         for chip in range(others):
@@ -395,25 +413,34 @@
     def ret_copy(i, owner, where):
         return remote(ret_out.at[i], ret_in.at[owner], ret_send, ret_recv.at[owner], at(where))
 
-    def col_copy(k):
-        return remote(col_out.at[peer(k)], col_in.at[s], ret_send, col_recv, {"sub": peer(k)})
+    def columns_of(b):
+        where = pl.ds(pl.multiple_of(b * rows, rows), rows)
+        return jnp.max(col_part[:, where], axis=0, keepdims=True)
+
+    def send_columns(b):
+        col_out[b] = columns_of(b)
+        remote(col_out.at[b], col_in.at[s], ret_send, col_recv, {"sub": b}).start()
 
     def give(i):
         ret_out[i] = flat(i)
         ret_copy(i, z, i).start()
 
+    def finish(parts, blocks):
+        for chip in range(1, others):
+            meet_rows(parts, chip)
+            for b in range(2):
+                send_columns(lax.rem(s // 2 + chip, others) * 2 + b)
+        meet_rows(parts, 0)
+        for i in blocks:
+            give(i)
+        send_columns(partner)
+
     half = rows // 2
 
-    @pl.when(z == 0)
+    @pl.when(z == last)
     def _():
         lax.fori_loop(
-            near0, chunks, lambda k, c: (own_along(k, z + 1, bulk_recv.at[rest0]).start(), c)[1], 0
-        )
-
-    @pl.when(z == last)
-    def _():
-        lax.fori_loop(
-            early1, early1 + far0, lambda j, c: (relay_step(j), c)[1], 0
+            their_early1, their_early1 + far0, lambda j, c: (relay_step(j), c)[1], 0
         )
         lax.fori_loop(
             ahead, chunks, lambda k, c: (own_along(k, z - 1, bulk_recv.at[block3]).start(), c)[1], 0
@@ -423,6 +450,13 @@
     def _():
         def early(p, carry):
             level_forward(p)
+
+            @pl.when((z == 0) & (p == REST0))
+            def _():
+                lax.fori_loop(
+                    near0, chunks,
+                    lambda k, c: (own_along(k, z + 1, second_recv.at[rest0]).start(), c)[1], 0,
+                )
 
             @pl.when(p == pieces // 2)
             def _():
@@ -445,14 +479,24 @@
             @pl.when(t < near0)
             def _():
                 passed_on(0, t, z, first_recv.at[t]).wait_recv()
+
+                @pl.when((rep == 1) & (t >= near0 - skip))
+                def _():
+                    passed_on(0, t, z + 2, second_recv.at[far0b]).start()
+
                 passed_on(0, t, z + 1, first_recv.at[t]).start()
 
             @pl.when(t == near0 - 1)
             def _():
-                lax.fori_loop(
-                    lead1, near1,
-                    lambda k, c: (own_along(k, z + 1, second_recv.at[k]).start(), c)[1], 0,
-                )
+                def late(k, carry):
+                    @pl.when((rep == 0) & (k >= near1 - skip))
+                    def _():
+                        own_along(k, z + 2, second_recv.at[far1_recv]).start()
+
+                    own_along(k, z + 1, second_recv.at[k]).start()
+                    return carry
+
+                lax.fori_loop(lead1, near1, late, 0)
 
         ticks(
             max(LAG1[0] * unit + far0 + max(FAR1) * unit, (LAG1[2] + 12) * unit + 1), native,
@@ -461,17 +505,27 @@
         )
         wait_home()
         wait_away()
+        spread(0, lane_ids[0])
+        wait_bulk(rest0, far0, second_recv)
+        finish(((0, 0, rows),), (0,))
         meet_all(z, 0, rows, True)
-        spread(0, lane_ids[0])
-        wait_bulk(rest0, far0)
-        meet_all(0, 0, rows)
-        give(0)
 
     @pl.when(z == pivot)
     def _():
         ids_on(1, z).wait_recv()
         ids_on(1, z + 1).start()
         lead = LAG2[4] * unit
+
+        def meet_first():
+            spread(0, lane_ids[0])
+            wait_bulk(back0, far0)
+            meet_all(0, 0, rows)
+            give(0)
+
+        def own_away():
+            for chip in range(1, others):
+                meet(z, 0, rows, chip, True)
+
         steps = near1 + near0
 
         def native(t):
@@ -483,7 +537,10 @@
             @pl.when((k >= 0) & (k < lead1) | (k >= lead1 + near0) & (k < steps))
             def _():
                 passed_on(1, own, z, second_recv.at[own]).wait_recv()
-                passed_on(1, own, z + 1, bulk_recv.at[far1_recv]).start()
+
+                @pl.when((rep == 1) | (own < near1 - skip))
+                def _():
+                    passed_on(1, own, z + 1, second_recv.at[far1_recv]).start()
 
             @pl.when(m == 0)
             def _():
@@ -496,41 +553,58 @@
 
             @pl.when((m >= 0) & (m < chunks // 2))
             def _():
-                passed_on(0, m, z + 1, bulk_recv.at[far0a]).start()
-
-            @pl.when((m >= chunks // 2) & (m < near0))
-            def _():
-                passed_on(0, m, z + 1, bulk_recv.at[far0b]).start()
-
-            @pl.when(k == steps - 9 * unit)
+                passed_on(0, m, z + 1, second_recv.at[far0a]).start()
+
+            @pl.when((m >= chunks // 2) & (m < near0 - skip * rep))
+            def _():
+                passed_on(0, m, z + 1, second_recv.at[far0b]).start()
+
+            @pl.when(k == steps - unit * (HOME[0] * (1 - rep) + HOME[1] * rep))
             def _():
                 wait_home()
                 meet(z, 0, rows, 0, True)
 
-            @pl.when(k == steps - 2 * unit)
+            @pl.when((k == steps - 2 * unit) & (rep == 0))
             def _():
                 wait_away()
-                for chip in range(1, others):
-                    meet(z, 0, rows, chip, True)
+                meet_first()
+
+            @pl.when((k == steps - 2 * unit) & (rep == 1))
+            def _():
+                wait_away()
+                own_away()
 
         ticks(
             steps + lead, native,
             unit * (LAG2[0] * (1 - rep) + LAG2[1] * rep),
             unit * (LAG2[2] * (1 - rep) + LAG2[3] * rep),
         )
-        spread(0, lane_ids[0])
-        wait_bulk(back0, far0)
-        meet_all(0, 0, rows)
-        give(0)
+        def await_last():
+            ids_on(last, z).wait_recv()
+            spread(last, lane_ids[last])
+            wait_bulk(block3, chunks)
+
+        @pl.when(rep == 1)
+        def _():
+            await_last()
+            meet_all(last, 0, rows)
+            give(last)
+            meet_first()
+
         spread(1, lane_ids[1])
         either_way(lambda far: wait_bulk(back1, far))
-        meet_all(1, 0, rows)
-        give(1)
-        ids_on(last, z).wait_recv()
-        spread(last, lane_ids[last])
-        wait_bulk(block3, chunks)
-        meet_all(last, 0, rows)
-        give(last)
+
+        @pl.when(rep == 0)
+        def _():
+            meet_all(1, 0, rows)
+            give(1)
+            await_last()
+            finish(((last, 0, rows),), (last,))
+            own_away()
+
+        @pl.when(rep == 1)
+        def _():
+            finish(((1, 0, rows),), (1,))
 
     @pl.when(z == last)
     def _():
@@ -538,23 +612,37 @@
         spread(0, lane_ids[0])
         ids_on(1, z).wait_recv()
         spread(1, lane_ids[1])
-        wait_bulk(far0a, chunks // 2)
-        meet_all(0, 0, half)
-        wait_bulk(far0b, near0 - chunks // 2)
-        wait_bulk(back0, far0)
-        meet_all(0, half, rows)
-        give(0)
-        either_way(lambda far: wait_bulk(back1, far))
-        either_way(lambda far: wait_bulk(far1_recv, chunks - far))
-        meet_all(1, 0, rows)
-        give(1)
-
-    @pl.when(z > 0)
-    def _():
-        for b in range(subgroup):
-            col_out[b] = jnp.max(col_part[:, b * rows : (b + 1) * rows], axis=0, keepdims=True)
-        for k in range(1, subgroup):
-            col_copy(k).start()
+
+        def first_half():
+            wait_bulk(far0a, chunks // 2, second_recv)
+            meet_all(0, 0, half)
+
+        def await_second_half():
+            wait_bulk(far0b, near0 - chunks // 2, second_recv)
+            wait_bulk(back0, far0)
+
+        @pl.when(rep == 0)
+        def _():
+            first_half()
+            await_second_half()
+            meet_all(0, half, rows)
+            give(0)
+            wait_bulk(back1, FAR1[0] * unit)
+            wait_bulk(far1_recv, chunks - FAR1[0] * unit, second_recv)
+            meet_all(1, 0, rows)
+            give(1)
+            for k in range(1, subgroup):
+                send_columns(peer(k))
+
+        @pl.when(rep == 1)
+        def _():
+            near = chunks - FAR1[1] * unit
+            wait_bulk(far1_recv, near, second_recv)
+            meet_all(1, 0, near * size)
+            first_half()
+            await_second_half()
+            wait_bulk(back1, FAR1[1] * unit)
+            finish(((0, half, rows), (1, near * size, rows)), (1, 0))
 
     out_ref[...] = flat(z).reshape(rows)
 
@@ -576,17 +664,21 @@
     def _():
         bytes_of((chunks + far0) * size, own_send, col_recv).wait_send()
 
-    @pl.when((z == 1) | (z == last))
+    @pl.when(z == 1)
+    def _():
+        for way in (0, 1):
+            @pl.when(rep == way)
+            def _(way=way):
+                bytes_of((chunks + skip * (1 - way)) * size, own_send, col_recv).wait_send()
+                bytes_of((near0 + skip * way) * size, pass_send, col_recv).wait_send()
+
+    @pl.when(z == last)
     def _():
         bytes_of(rows, own_send, col_recv).wait_send()
-
-    @pl.when(z == last)
-    def _():
         bytes_of(far0 * size, relay_send, col_recv).wait_send()
 
     @pl.when(z == 1)
     def _():
-        bytes_of((chunks - far0) * size, pass_send, col_recv).wait_send()
         either_way(
             lambda far: bytes_of(
                 2 * (far0 + sum(FAR1) * unit - far) * size, relay_send, col_recv
@@ -596,7 +688,7 @@
     @pl.when(z == pivot)
     def _():
         either_way(
-            lambda far: bytes_of((chunks - far + near0) * size, pass_send, col_recv).wait_send()
+            lambda far: bytes_of((chunks - far - skip + near0) * size, pass_send, col_recv).wait_send()
         )
         either_way(
             lambda far: bytes_of(
@@ -608,7 +700,7 @@
     def _():
         block = col_in.at[pl.ds(0, subgroup - 1)]
         remote(block, block, ret_send, col_recv, {"sub": peer(1)}).wait_recv()
-        heard = col_out[s]
+        heard = columns_of(s)
         for k in range(1, subgroup):
             heard = jnp.maximum(heard, col_in[peer(k)])
         out_ref[...] = jnp.maximum(out_ref[...], heard.reshape(rows))
@@ -655,7 +747,7 @@
             pltpu.VMEM((2 * subgroup, 1, rows), jnp.float32),
             dma((pieces,)), dma, dma, dma((groups,)), dma,
             dma, dma((max(subgroup // 2 - 1, 1), pieces)), dma((2,)), dma, dma, dma,
-            dma((3 * chunks // 4,)), dma((chunks - min(FAR1) * chunks // 16,)), dma((7,)),
+            dma((3 * chunks // 4,)), dma((chunks - min(FAR1) * chunks // 16,)), dma((3,)),
             dma((chunks // 4 + max(FAR1) * chunks // 16,)),
             dma, dma((groups,)), dma,
         ],

time: 27.2 us -> 26.8 us (0.985)
  Pallas kernels: 26.5 us -> 26.1 us
    pallas_call x1, Pallas kernels: 26.5 us -> 26.1 us  [by_meeting(): pl.pallas_call(functools.partial(meet_kernel, groups, subgroup, chunks, p...]
where the time goes in v4:
time: 26.8 us; the launch traced here: 26.6 us
  Pallas kernels  26.1 us (97%)
  local copies, waits for them, and re-layouts  0.56 us (2%)
    pallas_call x1, Pallas kernels, by_meeting(): pl.pallas_call(functools.partial(meet_kernel, groups, subgroup, chunks, p...  26.1 us
    unnamed x1, local copies, waits for them, and re-layouts  0.56 us

profile of v4, /device:TPU:0, one launch (start us, length us, event | category | flops | bytes accessed | tf_op | source)
XLA Modules:
  0.0 26.6 jit_solution(17576827123859299751)
XLA Ops:
  0.0 26.1 %shard_map.28 = f32[256]{0:T(256)S(1)} custom-call(bf16[256,1024]{1,0:T(8,128)(2,1)} %emb_ref.1, s32[1,256]{1,0:T(1,128)} %bitcast.1), custom_call_target="tpu_custom_call" | custom-call | tf_op jit(solution)/shard_map/pallas_call | solution.py:729
  26.1 0.6 %copy.4 = f32[256]{0:T(256)} copy(f32[256]{0:T(256)S(1)} %shard_map.28) | data formatting | bytes 2048

commit v5 on v4

--- a/solution.py
+++ b/solution.py
@@ -102,7 +102,7 @@
     ret_out, ret_in, col_out, col_in,
     in_sem, ids_in, ids_send, ids_recv, lid_recv,
     lvl_send, lvl_recv, mate_recv, own_send, pass_send, relay_send,
-    first_recv, second_recv, bulk_recv, relay_recv, ret_send, ret_recv, col_recv,
+    first_recv, second_recv, bulk_recv, relay_recv, ret_send, col_recv,
 ):
     rows, features = emb_ref.shape
     size = rows // chunks
@@ -160,27 +160,29 @@
     def turned(p):
         return lax.rem(p + turn, pieces)
 
-    for p in range(pieces):
+    load_piece(turned(0)).start()
+    barrier = pltpu.get_barrier_semaphore()
+
+    @pl.when(z > 0)
+    def _():
+        pl.semaphore_signal(barrier, 1, device_id=at(z - 1), device_id_type=MESH)
+
+    @pl.when(z < last)
+    def _():
+        pl.semaphore_signal(barrier, 1, device_id=at(z + 1), device_id_type=MESH)
+
+    @pl.when(z == last)
+    def _():
+        pl.semaphore_signal(barrier, 1, device_id=at(z - 1) | across_y, device_id_type=MESH)
+
+    pl.semaphore_signal(barrier, 1, device_id=across_y, device_id_type=MESH)
+    for k in range(1, subgroup):
+        pl.semaphore_signal(barrier, 1, device_id={"sub": peer(k)}, device_id_type=MESH)
+
+    for p in range(1, pieces):
         load_piece(turned(p)).start()
     ids_copy = pltpu.make_async_copy(ids_ref, level_ids.at[s], ids_in)
     ids_copy.start()
-
-    barrier = pltpu.get_barrier_semaphore()
-    for k in range(1, subgroup):
-        pl.semaphore_signal(barrier, 1, device_id={"sub": peer(k)}, device_id_type=MESH)
-    pl.semaphore_signal(barrier, 1, device_id=across_y, device_id_type=MESH)
-
-    @pl.when(z > 0)
-    def _():
-        pl.semaphore_signal(barrier, 1, device_id=at(z - 1), device_id_type=MESH)
-
-    @pl.when(z < last)
-    def _():
-        pl.semaphore_signal(barrier, 1, device_id=at(z + 1), device_id_type=MESH)
-
-    @pl.when(z == last)
-    def _():
-        pl.semaphore_signal(barrier, 1, device_id=at(z - 1) | across_y, device_id_type=MESH)
 
     col_part[...] = jnp.full(col_part.shape, -1.0, jnp.float32)
     row_part[...] = jnp.full(row_part.shape, -1.0, jnp.float32)
@@ -276,18 +278,18 @@
     )
     neighbours = subgroup + sum(c.astype(jnp.int32) for c in (z > 0, z < last, z == 1))
     pl.semaphore_wait(barrier, neighbours)
+
+    @pl.when(sends_right)
+    def _():
+        own_ids(z + 1).start()
+
+    @pl.when(sends_left)
+    def _():
+        own_ids(z - 1).start()
+
+    send_own(turn)
     for k in range(1, subgroup):
         level_ids_copy(k).start()
-
-    @pl.when(sends_right)
-    def _():
-        own_ids(z + 1).start()
-
-    @pl.when(sends_left)
-    def _():
-        own_ids(z - 1).start()
-
-    send_own(turn)
 
     def norm_step(q, carry):
         p = turned(q)
@@ -299,7 +301,8 @@
     lax.fori_loop(1, pieces, norm_step, 0)
     ids_copy.wait()
 
-    def level_forward(p):
+    def level_forward(q):
+        p = turned(q)
         for k in range(1, others):
             arrived = level_piece(peer(subgroup - 2 * k), p, lvl_recv.at[k - 1, p], s)
             arrived.wait_recv()
@@ -411,7 +414,7 @@
         return jnp.max(row_part[i].T, axis=0, keepdims=True)
 
     def ret_copy(i, owner, where):
-        return remote(ret_out.at[i], ret_in.at[owner], ret_send, ret_recv.at[owner], at(where))
+        return remote(ret_out.at[i], ret_in.at[owner], ret_send, second_recv.at[groups + owner], at(where))
 
     def columns_of(b):
         where = pl.ds(pl.multiple_of(b * rows, rows), rows)
@@ -747,9 +750,9 @@
             pltpu.VMEM((2 * subgroup, 1, rows), jnp.float32),
             dma((pieces,)), dma, dma, dma((groups,)), dma,
             dma, dma((max(subgroup // 2 - 1, 1), pieces)), dma((2,)), dma, dma, dma,
-            dma((3 * chunks // 4,)), dma((chunks - min(FAR1) * chunks // 16,)), dma((3,)),
+            dma((3 * chunks // 4,)), dma((max(chunks - min(FAR1) * chunks // 16, 2 * groups),)), dma((3,)),
             dma((chunks // 4 + max(FAR1) * chunks // 16,)),
-            dma, dma((groups,)), dma,
+            dma, dma,
         ],
         compiler_params=pltpu.CompilerParams(collective_id=0, has_side_effects=True),
     )(embeddings, cluster_ids.reshape(1, rows))

time: 26.8 us -> 26.7 us (level)
  no operation moved by 1% of the time
where the time goes in v5:
time: 26.7 us; the launch traced here: 26.5 us
  Pallas kernels  25.9 us (97%)
  local copies, waits for them, and re-layouts  0.56 us (2%)
    pallas_call x1, Pallas kernels, by_meeting(): pl.pallas_call(functools.partial(meet_kernel, groups, subgroup, chunks, p...  25.9 us
    unnamed x1, local copies, waits for them, and re-layouts  0.56 us

profile of v5, /device:TPU:0, one launch (start us, length us, event | category | flops | bytes accessed | tf_op | source)
XLA Modules:
  0.0 26.5 jit_solution(3400332328093235707)
XLA Ops:
  0.0 25.9 %shard_map.28 = f32[256]{0:T(256)S(1)} custom-call(bf16[256,1024]{1,0:T(8,128)(2,1)} %emb_ref.1, s32[1,256]{1,0:T(1,128)} %bitcast.1), custom_call_target="tpu_custom_call" | custom-call | tf_op jit(solution)/shard_map/pallas_call | solution.py:732
  26.0 0.6 %copy.4 = f32[256]{0:T(256)} copy(f32[256]{0:T(256)S(1)} %shard_map.28) | data formatting | bytes 2048

commit v6 on v5

--- a/solution.py
+++ b/solution.py
@@ -85,7 +85,7 @@
 
 
 LAG1 = (7, 4, 4, 4)
-LAG2 = (1, 0, 4, 4, 2)
+LAG2 = (1, 0, 4, 4, 1)
 REST0 = 1
 HOME = (5, 9)
 LEAD = (3, 7)

time: 26.7 us -> 26.7 us (level)
  no operation moved by 1% of the time
where the time goes in v6:
time: 26.7 us; the launch traced here: 26.5 us
  Pallas kernels  25.9 us (97%)
  local copies, waits for them, and re-layouts  0.56 us (2%)
    pallas_call x1, Pallas kernels, by_meeting(): pl.pallas_call(functools.partial(meet_kernel, groups, subgroup, chunks, p...  25.9 us
    unnamed x1, local copies, waits for them, and re-layouts  0.56 us

profile of v6, /device:TPU:0, one launch (start us, length us, event | category | flops | bytes accessed | tf_op | source)
XLA Modules:
  0.0 26.5 jit_solution(8572762560677320941)
XLA Ops:
  0.0 25.9 %shard_map.28 = f32[256]{0:T(256)S(1)} custom-call(bf16[256,1024]{1,0:T(8,128)(2,1)} %emb_ref.1, s32[1,256]{1,0:T(1,128)} %bitcast.1), custom_call_target="tpu_custom_call" | custom-call | tf_op jit(solution)/shard_map/pallas_call | solution.py:732
  26.0 0.6 %copy.4 = f32[256]{0:T(256)} copy(f32[256]{0:T(256)S(1)} %shard_map.28) | data formatting | bytes 2048

commit v7 on v6

--- a/solution.py
+++ b/solution.py
@@ -91,7 +91,7 @@
 LEAD = (3, 7)
 FAR1 = (7, 9)
 EARLY1 = (4, 6)
-AHEAD = (6, 4)
+AHEAD = (5, 3)
 SKIP = 1
 
 

time: 26.7 us -> 26.7 us (level)
  no operation moved by 1% of the time
where the time goes in v7:
time: 26.7 us; the launch traced here: 26.5 us
  Pallas kernels  25.9 us (97%)
  local copies, waits for them, and re-layouts  0.56 us (2%)
    pallas_call x1, Pallas kernels, by_meeting(): pl.pallas_call(functools.partial(meet_kernel, groups, subgroup, chunks, p...  25.9 us
    unnamed x1, local copies, waits for them, and re-layouts  0.56 us

profile of v7, /device:TPU:0, one launch (start us, length us, event | category | flops | bytes accessed | tf_op | source)
XLA Modules:
  0.0 26.5 jit_solution(12232386750280851421)
XLA Ops:
  0.0 25.9 %shard_map.28 = f32[256]{0:T(256)S(1)} custom-call(bf16[256,1024]{1,0:T(8,128)(2,1)} %emb_ref.1, s32[1,256]{1,0:T(1,128)} %bitcast.1), custom_call_target="tpu_custom_call" | custom-call | tf_op jit(solution)/shard_map/pallas_call | solution.py:732
  26.0 0.6 %copy.4 = f32[256]{0:T(256)} copy(f32[256]{0:T(256)S(1)} %shard_map.28) | data formatting | bytes 2048
